TPU v7x, 32 devices: a whole 2x2x4 slice. The times are simulated.
32 devices in a mesh: tm: 8 (over y, x, core), space: 4 (over z).
Axes of the slice: x: 2, y: 2, z: 4, core: 2. Of those that a mesh axis runs over, the one named last changes fastest.
Arguments:
- start_state: float32 [6, 2048], P(None, 'space'), may hold values from -6 to 6, as said below
- fine_nodes: float32 [8, 3, 6, 2048], P('tm', None, None, 'space'), may hold values from -8 to 8, as said below
Outputs:
- new_places: float32 [8, 3, 3, 2048], P('tm', None, None, 'space')
- new_strengths: float32 [8, 3, 3, 2048], P('tm', None, None, 'space')
- next_places: float32 [8, 3, 2048], P('tm', None, 'space')
- next_strengths: float32 [8, 3, 2048], P('tm', None, 'space')
Inputs may be any that keep to these rules, and one draw needn't show every extreme that they name: `start_state`: rows 0 to 2 are positions within the box from -0.5 to 0.5 give or take 0.05; the particles are numbered along a Morton (Z-order) curve of the box, so that runs of consecutive particles lie close together. `fine_nodes`: rows 0 to 2 are positions within the box from -0.5 to 0.5 give or take 0.1, numbered along the same Morton curve as start_state.
All inputs are finite; a program needn't handle non-finite values.
Results may differ from a plain program's by a relative error of at most 0.0003.
Values sent between devices are 32-bit elements; how exact they have to be, the bound alone decides.
A program may use at most 64 MiB of HBM per device.

v0:
```python
import functools
import math

import jax
import jax.numpy as jnp
from jax import lax
from jax.experimental import pallas as pl
from jax.experimental.pallas import tpu as pltpu
from jax.sharding import PartitionSpec as P

CLUSTER = 16

core_squared = 0.01
step_length = 0.02


def rounded(value):
    return value.astype(jnp.bfloat16).astype(jnp.float32)


def split_three(value):
    one = rounded(value)
    two = rounded(value - one)
    return one, two, rounded(value - one - two)


def split_two(value):
    high = value.astype(jnp.bfloat16)
    return high, (value - high.astype(jnp.float32)).astype(jnp.bfloat16)


def product(left, right):
    return jnp.dot(left, right, preferred_element_type=jnp.float32)


def pad_rows(value):
    return jnp.concatenate([value, jnp.zeros((8 - value.shape[0], value.shape[1]), value.dtype)], axis=0)


def place_parts(state, extra):
    high = rounded(state[0:3])
    low = rounded(state[0:3] - high)
    used = high + low
    norm = used[0:1] * used[0:1] + used[1:2] * used[1:2] + used[2:3] * used[2:3] + extra
    return high, low, split_three(norm)


def source_places(state):
    high, low, norm = place_parts(state, 0.0)
    ones = jnp.ones_like(norm[0])
    none = jnp.zeros_like(norm[0])
    return jnp.concatenate(
        [high, norm[0], norm[1], norm[2], ones, ones]
        + [low, ones, none, none, none, none]
        + [high, none, none, none, none, none]
        + [low, none, none, none, none, none],
        axis=0,
    ).astype(jnp.bfloat16)


def target_places(state):
    high, low, norm = place_parts(state, core_squared)
    high = -2.0 * high
    low = -2.0 * low
    ones = jnp.ones_like(norm[0])
    none = jnp.zeros_like(norm[0])
    return jnp.concatenate(
        [high, ones, ones, ones, norm[0], norm[1]]
        + [high, norm[2], none, none, none, none]
        + [low, none, none, none, none, none]
        + [low, none, none, none, none, none],
        axis=0,
    ).astype(jnp.bfloat16)


def cross(left, right):
    return jnp.concatenate(
        [
            left[1:2] * right[2:3] - left[2:3] * right[1:2],
            left[2:3] * right[0:1] - left[0:1] * right[2:3],
            left[0:1] * right[1:2] - left[1:2] * right[0:1],
        ],
        axis=0,
    )


def source_moments(state):
    base = pad_rows(jnp.concatenate([state[3:6], cross(state[0:3], state[3:6])], axis=0))
    whole = jnp.concatenate([base, state[0:1] * base, state[1:2] * base, state[2:3] * base], axis=0)
    parts = split_three(whole)
    for_q = jnp.concatenate([part[0:8] for part in parts] + [jnp.zeros_like(base)], axis=0)
    for_q = for_q.astype(jnp.bfloat16)
    for_h = jnp.concatenate(parts, axis=0).astype(jnp.bfloat16)
    return for_q, for_h


def pair_sums(places, for_q, for_h, target, both=True):
    count = target.shape[1]
    sum_q = jnp.zeros((8, count), jnp.float32)
    sum_h = jnp.zeros((32, count), jnp.float32)
    length = places.shape[1]
    piece = math.gcd(length, 256)
    for begin in range(0, length, piece):
        part = slice(begin, begin + piece)
        spread = lax.dot_general(
            places[:, part], target, (((0,), (0,)), ((), ())), preferred_element_type=jnp.float32
        )
        inverse = lax.rsqrt(spread)
        square = inverse * inverse
        factor = square * inverse
        steep = factor * square
        factor_high, factor_low = split_two(factor)
        steep_high, steep_low = split_two(steep)
        got_q = product(for_q[:, part], factor_high)
        got_h = product(for_h[:, part], steep_high)
        rest_q = got_q[8:16] + got_q[16:24]
        rest_h = got_h[32:64] + got_h[64:96]
        if both:
            rest_q = rest_q + product(for_q[0:16, part], factor_low)[0:8]
            rest_h = rest_h + product(for_h[0:32, part], steep_low)
        sum_q = sum_q + (got_q[0:8] + rest_q)
        sum_h = sum_h + (got_h[0:32] + rest_h)
    return jnp.concatenate([sum_q, sum_h], axis=0)


def finish(sums, state, coupling):
    places = state[0:3]
    strengths = state[3:6]
    weighted = sums[0:3]
    velocity = cross(places, weighted) - sums[3:6]
    along = (
        strengths[0:1] * places[0:1] + strengths[1:2] * places[1:2] + strengths[2:3] * places[2:3]
    )
    moment = 3.0 * (
        along * sums[8:16]
        - strengths[0:1] * sums[16:24]
        - strengths[1:2] * sums[24:32]
        - strengths[2:3] * sums[32:40]
    )
    stretch = cross(strengths, weighted) - (cross(places, moment[0:3]) - moment[3:6])
    return -coupling * jnp.concatenate([velocity, stretch], axis=0)


def kernel(
    n_t,
    n_s,
    start_ref,
    nodes_ref,
    places_out,
    strengths_out,
    next_places_out,
    next_strengths_out,
    gathered,
    sums,
    steps,
    history,
    coarse,
    middles,
    handed,
    pool,
    send_a,
    recv_a,
    send_b,
    recv_b,
    send_d,
    recv_d,
    send_e,
    recv_e,
    send_w,
    recv_w,
    send_h,
    recv_h,
):
    length = start_ref.shape[1]
    coupling = 1.0 / (4.0 * math.pi * math.sqrt(length * n_s))
    mine = lax.axis_index("tm")
    me = lax.axis_index("space")

    def space_copy(source, target, send, recv, peer):
        return pltpu.make_async_remote_copy(
            src_ref=source, dst_ref=target, send_sem=send, recv_sem=recv,
            device_id={"space": peer}, device_id_type=pl.DeviceIdType.MESH,
        )

    def time_copy(source, target, send, recv, peer):
        return pltpu.make_async_remote_copy(
            src_ref=source, dst_ref=target, send_sem=send, recv_sem=recv,
            device_id={"tm": peer}, device_id_type=pl.DeviceIdType.MESH,
        )

    lanes = nodes_ref.shape[1]
    pieces = length // lanes

    def put(target, row, value):
        for one in range(value.shape[0]):
            for piece in range(pieces):
                target[row + one, piece : piece + 1, :] = value[
                    one : one + 1, piece * lanes : (piece + 1) * lanes
                ]

    barrier = pltpu.get_barrier_semaphore()
    for offset in range(1, n_s):
        pl.semaphore_signal(
            barrier, inc=1, device_id={"space": lax.rem(me + offset, n_s)},
            device_id_type=pl.DeviceIdType.MESH,
        )
    for offset in range(1, n_t):
        pl.semaphore_signal(
            barrier, inc=1, device_id={"tm": lax.rem(mine + offset, n_t)},
            device_id_type=pl.DeviceIdType.MESH,
        )
    for node in range(3):
        for row in range(6):
            for piece in range(pieces):
                at = (node * 6 + row) * pieces + piece
                gathered[me, node, row : row + 1, piece * lanes : (piece + 1) * lanes] = nodes_ref[
                    at : at + 1, :
                ]
    pl.semaphore_wait(barrier, n_s - 1 + n_t - 1)

    def node_copy(offset, slot):
        return space_copy(
            gathered.at[me], gathered.at[slot], send_a.at[offset], recv_a.at[offset],
            lax.rem(me + offset, n_s),
        )

    def start_copy(offset, slot):
        return space_copy(
            start_ref, history.at[0, slot], send_b.at[offset], recv_b.at[offset],
            lax.rem(me + offset, n_s),
        )

    for offset in range(1, n_s):
        node_copy(offset, me).start()
    for offset in range(1, n_s):
        start_copy(offset, me).start()
    history[0, me] = start_ref[...]

    total = n_s * length
    clusters = total // CLUSTER
    particle = lax.broadcasted_iota(jnp.int32, (total, clusters), 0)
    cluster = lax.broadcasted_iota(jnp.int32, (total, clusters), 1)
    offset_in = particle - cluster * CLUSTER
    pool[...] = jnp.where((offset_in >= 0) & (offset_in < CLUSTER), 1.0, 0.0).astype(jnp.bfloat16)

    def aggregate(blocks):
        state = pad_rows(jnp.concatenate(blocks, axis=1))
        parts = jnp.concatenate(split_three(state), axis=0).astype(jnp.bfloat16)
        got = jnp.dot(parts, pool[...], preferred_element_type=jnp.float32)
        whole = got[0:8] + got[8:16] + got[16:24]
        return jnp.concatenate([whole[0:3] * (1.0 / CLUSTER), whole[3:6]], axis=0)

    def coarse_sources(blocks):
        merged = aggregate(blocks)
        return (source_places(merged),) + source_moments(merged)

    def fine_sums(source, target, both=True):
        for_q, for_h = source_moments(source)
        return pair_sums(source_places(source), for_q, for_h, target_places(target), both)

    for offset in range(n_s):
        source = lax.rem(me + n_s - offset, n_s)
        if offset > 0:
            node_copy(offset, source).wait_recv()

        def one_node(node, carry):
            got = fine_sums(gathered[source, node], gathered[me, node])
            if offset == 0:
                sums[node] = got
            else:
                sums[node] = sums[node] + got
            return carry

        lax.fori_loop(0, 3, one_node, 0)

    fine = [finish(sums[node], gathered[me, node], coupling) for node in range(3)]

    def coarse_value(blocks, target):
        return finish(pair_sums(*coarse_sources(blocks), target_places(target)), target, coupling)

    coarse_first = coarse_value([gathered[z, 0] for z in range(n_s)], gathered[me, 0])
    coarse_last = coarse_value([gathered[z, 2] for z in range(n_s)], gathered[me, 2])
    correction = step_length * (
        (fine[0] + 4.0 * fine[1] + fine[2]) / 6.0 - 0.5 * (coarse_first + coarse_last)
    )
    steps[mine, me] = correction + step_length * 0.5 * (coarse_last - coarse_first)

    def step_copy(offset, slot):
        return space_copy(
            steps.at[mine, me], steps.at[mine, slot], send_d.at[offset], recv_d.at[offset],
            lax.rem(me + offset, n_s),
        )

    for offset in range(1, n_s):
        step_copy(offset, me).start()
    for offset in range(1, n_s):
        start_copy(offset, lax.rem(me + n_s - offset, n_s)).wait_recv()
    for offset in range(1, n_s):
        step_copy(offset, lax.rem(me + n_s - offset, n_s)).wait_recv()

    def slice_copy(offset, slot):
        return time_copy(
            steps.at[slot], steps.at[slot], send_e.at[offset], recv_e.at[offset],
            lax.rem(mine + offset, n_t),
        )

    for offset in range(1, n_t):
        slice_copy(offset, mine).start()

    def chain_step(step, carry):
        sources = coarse_sources([history[step, z] for z in range(n_s)])

        @pl.when(step != mine)
        def _():
            slice_copy(lax.rem(mine + n_t - step, n_t), step).wait_recv()

        def one_block(z, inner):
            state = history[step, z]
            value = finish(pair_sums(*sources, target_places(state)), state, coupling)
            coarse[step, z] = value
            history[step + 1, z] = state + step_length * value + steps[step, z]
            return inner

        lax.fori_loop(0, n_s, one_block, 0, unroll=math.gcd(n_s, 4))
        return carry

    lax.fori_loop(0, n_t, chain_step, 0)

    initial = history[mine, me]
    final_state = history[mine + 1, me]
    coarse_end = coarse_value([history[mine + 1, z] for z in range(n_s)], final_state)
    change_first = coarse[mine, me] - coarse_first
    change_last = coarse_end - coarse_last
    fixed_first = fine[0] + change_first
    fixed_middle = fine[1] + 0.5 * (change_first + change_last)
    fixed_last = fine[2] + change_last

    sums[0] = jnp.zeros(sums.shape[1:], jnp.float32)

    def initial_block(z, carry):
        sums[0] = sums[0] + fine_sums(history[mine, z], history[mine, me], False)
        return carry

    lax.fori_loop(0, n_s, initial_block, 0)
    slope_first = finish(sums[0], initial, coupling)
    sweep_middle = (
        initial
        + 0.5 * step_length * (slope_first - fixed_first)
        + step_length * (5.0 * fixed_first + 8.0 * fixed_middle - fixed_last) / 24.0
    )
    middles[me] = sweep_middle

    def middle_copy(offset, slot):
        return space_copy(
            middles.at[me], middles.at[slot], send_w.at[offset], recv_w.at[offset],
            lax.rem(me + offset, n_s),
        )

    for offset in range(1, n_s):
        middle_copy(offset, me).start()
    put(places_out, 0, initial[0:3])
    put(strengths_out, 0, initial[3:6])
    put(places_out, 3, sweep_middle[0:3])
    put(strengths_out, 3, sweep_middle[3:6])
    sums[1] = fine_sums(sweep_middle, sweep_middle, False)
    for offset in range(1, n_s):
        source = lax.rem(me + n_s - offset, n_s)
        middle_copy(offset, source).wait_recv()
        sums[1] = sums[1] + fine_sums(middles[source], sweep_middle, False)
    slope_middle = finish(sums[1], sweep_middle, coupling)
    sweep_last = (
        sweep_middle
        + 0.5 * step_length * (slope_middle - fixed_middle)
        + step_length * (-fixed_first + 8.0 * fixed_middle + 5.0 * fixed_last) / 24.0
    )
    put(handed.at[0], 0, sweep_last)

    def last_copy():
        return time_copy(handed.at[0], handed.at[1], send_h, recv_h, lax.rem(mine + 1, n_t))

    @pl.when(mine < n_t - 1)
    def _():
        last_copy().start()

    places_out[6:9] = handed[0, 0:3]
    strengths_out[6:9] = handed[0, 3:6]
    for offset in range(1, n_s):
        node_copy(offset, me).wait_send()
        start_copy(offset, me).wait_send()
        step_copy(offset, me).wait_send()
        middle_copy(offset, me).wait_send()
    for offset in range(1, n_t):
        slice_copy(offset, mine).wait_send()

    @pl.when(mine == 0)
    def _():
        put(next_places_out, 0, start_ref[0:3])
        put(next_strengths_out, 0, start_ref[3:6])

    @pl.when(mine > 0)
    def _():
        last_copy().wait_recv()
        next_places_out[...] = handed[1, 0:3]
        next_strengths_out[...] = handed[1, 3:6]

    @pl.when(mine < n_t - 1)
    def _():
        last_copy().wait_send()


def solution(mesh):
    n_t, n_s = mesh.shape["tm"], mesh.shape["space"]

    def shards(start_state, fine_nodes):
        length = start_state.shape[1]
        total = length * n_s
        vmem = pl.BlockSpec(memory_space=pltpu.VMEM)
        dma = pltpu.SemaphoreType.DMA
        lanes = math.gcd(length, 128)
        rows = (length // lanes, lanes)
        results = pl.pallas_call(
            functools.partial(kernel, n_t, n_s),
            out_shape=(
                jax.ShapeDtypeStruct((9,) + rows, jnp.float32),
                jax.ShapeDtypeStruct((9,) + rows, jnp.float32),
                jax.ShapeDtypeStruct((3,) + rows, jnp.float32),
                jax.ShapeDtypeStruct((3,) + rows, jnp.float32),
            ),
            in_specs=[vmem, vmem],
            out_specs=(vmem, vmem, vmem, vmem),
            scratch_shapes=[
                pltpu.VMEM((n_s, 3, 6, length), jnp.float32),
                pltpu.VMEM((3, 40, length), jnp.float32),
                pltpu.VMEM((n_t, n_s, 6, length), jnp.float32),
                pltpu.VMEM((n_t + 1, n_s, 6, length), jnp.float32),
                pltpu.VMEM((n_t, n_s, 6, length), jnp.float32),
                pltpu.VMEM((n_s, 6, length), jnp.float32),
                pltpu.VMEM((2, 6) + rows, jnp.float32),
                pltpu.VMEM((total, total // CLUSTER), jnp.bfloat16),
                dma((n_s,)), dma((n_s,)),
                dma((n_s,)), dma((n_s,)),
                dma((n_s,)), dma((n_s,)),
                dma((n_t,)), dma((n_t,)),
                dma((n_s,)), dma((n_s,)),
                dma, dma,
            ],
            compiler_params=pltpu.CompilerParams(collective_id=0, has_side_effects=True),
        )(start_state, fine_nodes.reshape(-1, lanes))
        nodes, ends = (1, 3, 3, length), (1, 3, length)
        return tuple(
            one.reshape(shape) for one, shape in zip(results, (nodes, nodes, ends, ends))
        )

    return jax.shard_map(
        shards,
        mesh=mesh,
        in_specs=(P(None, "space"), P("tm", None, None, "space")),
        out_specs=(
            P("tm", None, None, "space"),
            P("tm", None, None, "space"),
            P("tm", None, "space"),
            P("tm", None, "space"),
        ),
        check_vma=False,
    )
```

profile of v0, /device:TPU:7, one launch (start us, length us, event | category | flops | bytes accessed | tf_op | source)
XLA Modules:
  0.0 56.4 jit_solution(18227764595979536705)
XLA Ops:
  0.6 52.4 %shard_map.57 = (f32[9,4,128]{2,1,0:T(4,128)}, f32[9,4,128]{2,1,0:T(4,128)}, f32[3,4,128]{2,1,0:T(4,128)}, f32[3,4,128]{2,1,0:T(4,128)}) custom-call(f32[6,512]{1,0:T(8,128)} %start_ref.1, f32[72,128]{1,0:T(8,128)} %bitcast.5), custom_call_target="tpu_custom_call" | custom-call | tf_op jit(solution)/shard_map/pallas_call | solution.py:421
  53.1 0.0 copy-start
  53.1 1.3 %copy.18 = f32[1,3,3,512]{3,0,2,1:T(1,128)} copy(f32[1,3,3,512]{3,0,2,1:T(1,128)} %bitcast.7) | data formatting | bytes 36864
  54.4 0.0 copy-done
  54.4 0.0 copy-start.2
  54.4 0.6 %copy.19 = f32[1,3,3,512]{3,0,2,1:T(1,128)} copy(f32[1,3,3,512]{3,0,2,1:T(1,128)S(1)} %bitcast.6) | data formatting | bytes 36864
  55.0 0.1 copy-done.2
  55.1 0.0 copy-start.1
  55.1 0.6 %copy.20 = f32[1,3,512]{2,0,1:T(1,128)} copy(f32[1,3,512]{2,0,1:T(1,128)S(1)} %bitcast.9) | data formatting | bytes 12288
  55.7 0.1 copy-done.1
  55.8 0.6 %copy.21 = f32[1,3,512]{2,0,1:T(1,128)} copy(f32[1,3,512]{2,0,1:T(1,128)S(1)} %bitcast.8) | data formatting | bytes 12288
Async XLA Ops:
  53.1 1.3 %copy-start = (f32[9,4,128]{2,1,0:T(4,128)S(1)}, f32[9,4,128]{2,1,0:T(4,128)}, u32[]{:S(2)}) copy-start(f32[9,4,128]{2,1,0:T(4,128)} %get-tuple-element.9) | copy-start | bytes 55300
  54.4 0.7 %copy-start.2 = (f32[3,4,128]{2,1,0:T(4,128)S(1)}, f32[3,4,128]{2,1,0:T(4,128)}, u32[]{:S(2)}) copy-start(f32[3,4,128]{2,1,0:T(4,128)} %get-tuple-element.10) | copy-start | bytes 18436
  55.1 0.7 %copy-start.1 = (f32[3,4,128]{2,1,0:T(4,128)S(1)}, f32[3,4,128]{2,1,0:T(4,128)}, u32[]{:S(2)}) copy-start(f32[3,4,128]{2,1,0:T(4,128)} %get-tuple-element.11) | copy-start | bytes 18436
where the time goes:
time: 56.8 us; the launch traced here: 56.4 us
  Pallas kernels  52.4 us (92%)
  local copies, waits for them, and re-layouts  3.33 us (6%)
  between operations  0.65 us (1%)
    pallas_call x1, Pallas kernels, shards(): pl.pallas_call(functools.partial(kernel, n_t, n_s), out_shape=(jax.ShapeD...  52.4 us
    unnamed x10, local copies, waits for them, and re-layouts  3.33 us

commit v1 on v0

--- a/solution.py
+++ b/solution.py
@@ -87,19 +87,17 @@
 def source_moments(state):
     base = pad_rows(jnp.concatenate([state[3:6], cross(state[0:3], state[3:6])], axis=0))
     whole = jnp.concatenate([base, state[0:1] * base, state[1:2] * base, state[2:3] * base], axis=0)
-    parts = split_three(whole)
-    for_q = jnp.concatenate([part[0:8] for part in parts] + [jnp.zeros_like(base)], axis=0)
-    for_q = for_q.astype(jnp.bfloat16)
-    for_h = jnp.concatenate(parts, axis=0).astype(jnp.bfloat16)
+    high, low = split_two(whole)
+    for_q = jnp.concatenate([high[0:8], low[0:8]], axis=0)
+    for_h = jnp.concatenate([high, low], axis=0)
     return for_q, for_h
 
 
 def pair_sums(places, for_q, for_h, target, both=True):
-    count = target.shape[1]
-    sum_q = jnp.zeros((8, count), jnp.float32)
-    sum_h = jnp.zeros((32, count), jnp.float32)
     length = places.shape[1]
     piece = math.gcd(length, 256)
+    parts_q, parts_h = [], []
+    left_q, left_h = [], []
     for begin in range(0, length, piece):
         part = slice(begin, begin + piece)
         spread = lax.dot_general(
@@ -109,18 +107,23 @@
         square = inverse * inverse
         factor = square * inverse
         steep = factor * square
-        factor_high, factor_low = split_two(factor)
-        steep_high, steep_low = split_two(steep)
-        got_q = product(for_q[:, part], factor_high)
-        got_h = product(for_h[:, part], steep_high)
-        rest_q = got_q[8:16] + got_q[16:24]
-        rest_h = got_h[32:64] + got_h[64:96]
         if both:
-            rest_q = rest_q + product(for_q[0:16, part], factor_low)[0:8]
-            rest_h = rest_h + product(for_h[0:32, part], steep_low)
-        sum_q = sum_q + (got_q[0:8] + rest_q)
-        sum_h = sum_h + (got_h[0:32] + rest_h)
-    return jnp.concatenate([sum_q, sum_h], axis=0)
+            parts_q.extend(split_two(factor))
+            parts_h.extend(split_two(steep))
+            left_q.extend([for_q[:, part]] * 2)
+            left_h.extend([for_h[:, part]] * 2)
+        else:
+            parts_q.append(factor.astype(jnp.bfloat16))
+            parts_h.append(steep.astype(jnp.bfloat16))
+            left_q.append(for_q[:, part])
+            left_h.append(for_h[:, part])
+
+    def total(left, right):
+        return product(jnp.concatenate(left, axis=1), jnp.concatenate(right, axis=0))
+
+    got_q = total(left_q, parts_q)
+    got_h = total(left_h, parts_h)
+    return jnp.concatenate([got_q[0:8] + got_q[8:16], got_h[0:32] + got_h[32:64]], axis=0)
 
 
 def finish(sums, state, coupling):
@@ -158,6 +161,7 @@
     middles,
     handed,
     pool,
+    spots,
     send_a,
     recv_a,
     send_b,
@@ -258,32 +262,28 @@
         for_q, for_h = source_moments(source)
         return pair_sums(source_places(source), for_q, for_h, target_places(target), both)
 
+    targets = [target_places(gathered[me, node]) for node in range(3)]
+    for node in range(3):
+        spots[node] = targets[node]
     for offset in range(n_s):
         source = lax.rem(me + n_s - offset, n_s)
         if offset > 0:
             node_copy(offset, source).wait_recv()
-
-        def one_node(node, carry):
-            got = fine_sums(gathered[source, node], gathered[me, node])
+        for node in range(3):
+            state = gathered[source, node]
+            got = pair_sums(source_places(state), *source_moments(state), spots[node], node == 1)
             if offset == 0:
                 sums[node] = got
             else:
                 sums[node] = sums[node] + got
-            return carry
-
-        lax.fori_loop(0, 3, one_node, 0)
 
     fine = [finish(sums[node], gathered[me, node], coupling) for node in range(3)]
 
-    def coarse_value(blocks, target):
-        return finish(pair_sums(*coarse_sources(blocks), target_places(target)), target, coupling)
-
-    coarse_first = coarse_value([gathered[z, 0] for z in range(n_s)], gathered[me, 0])
-    coarse_last = coarse_value([gathered[z, 2] for z in range(n_s)], gathered[me, 2])
-    correction = step_length * (
-        (fine[0] + 4.0 * fine[1] + fine[2]) / 6.0 - 0.5 * (coarse_first + coarse_last)
-    )
-    steps[mine, me] = correction + step_length * 0.5 * (coarse_last - coarse_first)
+    def coarse_value(blocks, target, both):
+        return finish(pair_sums(*coarse_sources(blocks), target_places(target), both), target, coupling)
+
+    coarse_first = coarse_value([gathered[z, 0] for z in range(n_s)], gathered[me, 0], True)
+    steps[mine, me] = step_length * ((fine[0] + 4.0 * fine[1] + fine[2]) / 6.0 - coarse_first)
 
     def step_copy(offset, slot):
         return space_copy(
@@ -295,6 +295,23 @@
         step_copy(offset, me).start()
     for offset in range(1, n_s):
         start_copy(offset, lax.rem(me + n_s - offset, n_s)).wait_recv()
+    coarse_last = coarse_value([gathered[z, 2] for z in range(n_s)], gathered[me, 2], False)
+
+    def coarse_step(step):
+        sources = coarse_sources([history[step, z] for z in range(n_s)])
+
+        def one_block(z, inner):
+            state = history[step, z]
+            coarse[step, z] = finish(pair_sums(*sources, target_places(state)), state, coupling)
+            return inner
+
+        lax.fori_loop(0, n_s, one_block, 0, unroll=math.gcd(n_s, 4))
+
+    def advance(step):
+        for z in range(n_s):
+            history[step + 1, z] = history[step, z] + step_length * coarse[step, z] + steps[step, z]
+
+    coarse_step(0)
     for offset in range(1, n_s):
         step_copy(offset, lax.rem(me + n_s - offset, n_s)).wait_recv()
 
@@ -305,30 +322,23 @@
         )
 
     for offset in range(1, n_t):
-        slice_copy(offset, mine).start()
+
+        @pl.when(mine + offset < n_t)
+        def _():
+            slice_copy(offset, mine).start()
 
     def chain_step(step, carry):
-        sources = coarse_sources([history[step, z] for z in range(n_s)])
-
-        @pl.when(step != mine)
-        def _():
-            slice_copy(lax.rem(mine + n_t - step, n_t), step).wait_recv()
-
-        def one_block(z, inner):
-            state = history[step, z]
-            value = finish(pair_sums(*sources, target_places(state)), state, coupling)
-            coarse[step, z] = value
-            history[step + 1, z] = state + step_length * value + steps[step, z]
-            return inner
-
-        lax.fori_loop(0, n_s, one_block, 0, unroll=math.gcd(n_s, 4))
+        slice_copy(mine - step, step).wait_recv()
+        advance(step)
+        coarse_step(step + 1)
         return carry
 
-    lax.fori_loop(0, n_t, chain_step, 0)
+    lax.fori_loop(0, mine, chain_step, 0)
+    advance(mine)
 
     initial = history[mine, me]
     final_state = history[mine + 1, me]
-    coarse_end = coarse_value([history[mine + 1, z] for z in range(n_s)], final_state)
+    coarse_end = coarse_value([history[mine + 1, z] for z in range(n_s)], final_state, False)
     change_first = coarse[mine, me] - coarse_first
     change_last = coarse_end - coarse_last
     fixed_first = fine[0] + change_first
@@ -390,7 +400,11 @@
         step_copy(offset, me).wait_send()
         middle_copy(offset, me).wait_send()
     for offset in range(1, n_t):
-        slice_copy(offset, mine).wait_send()
+
+        @pl.when(mine + offset < n_t)
+        def _():
+            slice_copy(offset, mine).wait_send()
+
 
     @pl.when(mine == 0)
     def _():
@@ -437,6 +451,7 @@
                 pltpu.VMEM((n_s, 6, length), jnp.float32),
                 pltpu.VMEM((2, 6) + rows, jnp.float32),
                 pltpu.VMEM((total, total // CLUSTER), jnp.bfloat16),
+                pltpu.VMEM((3, 32, length), jnp.bfloat16),
                 dma((n_s,)), dma((n_s,)),
                 dma((n_s,)), dma((n_s,)),
                 dma((n_s,)), dma((n_s,)),

time: 56.8 us -> 47 us (0.83)
  Pallas kernels: 52.4 us -> 42.7 us
    pallas_call x1, Pallas kernels: 52.4 us -> 42.7 us  [shards(): pl.pallas_call(functools.partial(kernel, n_t, n_s), out_shape=(jax.ShapeD...]
where the time goes in v1:
time: 47 us; the launch traced here: 46.7 us
  Pallas kernels  42.7 us (91%)
  local copies, waits for them, and re-layouts  3.33 us (7%)
  between operations  0.65 us (1%)
    pallas_call x1, Pallas kernels, shards(): pl.pallas_call(functools.partial(kernel, n_t, n_s), out_shape=(jax.ShapeD...  42.7 us
    unnamed x10, local copies, waits for them, and re-layouts  3.33 us

profile of v1, /device:TPU:7, one launch (start us, length us, event | category | flops | bytes accessed | tf_op | source)
XLA Modules:
  0.0 46.7 jit_solution(14571061990276648049)
XLA Ops:
  0.6 42.7 %shard_map.57 = (f32[9,4,128]{2,1,0:T(4,128)}, f32[9,4,128]{2,1,0:T(4,128)}, f32[3,4,128]{2,1,0:T(4,128)}, f32[3,4,128]{2,1,0:T(4,128)}) custom-call(f32[6,512]{1,0:T(8,128)} %start_ref.1, f32[72,128]{1,0:T(8,128)} %bitcast.5), custom_call_target="tpu_custom_call" | custom-call | tf_op jit(solution)/shard_map/pallas_call | solution.py:435
  43.4 0.0 copy-start
  43.4 1.3 %copy.18 = f32[1,3,3,512]{3,0,2,1:T(1,128)} copy(f32[1,3,3,512]{3,0,2,1:T(1,128)} %bitcast.7) | data formatting | bytes 36864
  44.7 0.0 copy-done
  44.7 0.0 copy-start.2
  44.7 0.6 %copy.19 = f32[1,3,3,512]{3,0,2,1:T(1,128)} copy(f32[1,3,3,512]{3,0,2,1:T(1,128)S(1)} %bitcast.6) | data formatting | bytes 36864
  45.3 0.1 copy-done.2
  45.4 0.0 copy-start.1
  45.4 0.6 %copy.20 = f32[1,3,512]{2,0,1:T(1,128)} copy(f32[1,3,512]{2,0,1:T(1,128)S(1)} %bitcast.9) | data formatting | bytes 12288
  46.0 0.1 copy-done.1
  46.1 0.6 %copy.21 = f32[1,3,512]{2,0,1:T(1,128)} copy(f32[1,3,512]{2,0,1:T(1,128)S(1)} %bitcast.8) | data formatting | bytes 12288
Async XLA Ops:
  43.4 1.3 %copy-start = (f32[9,4,128]{2,1,0:T(4,128)S(1)}, f32[9,4,128]{2,1,0:T(4,128)}, u32[]{:S(2)}) copy-start(f32[9,4,128]{2,1,0:T(4,128)} %get-tuple-element.9) | copy-start | bytes 55300
  44.7 0.7 %copy-start.2 = (f32[3,4,128]{2,1,0:T(4,128)S(1)}, f32[3,4,128]{2,1,0:T(4,128)}, u32[]{:S(2)}) copy-start(f32[3,4,128]{2,1,0:T(4,128)} %get-tuple-element.10) | copy-start | bytes 18436
  45.4 0.7 %copy-start.1 = (f32[3,4,128]{2,1,0:T(4,128)S(1)}, f32[3,4,128]{2,1,0:T(4,128)}, u32[]{:S(2)}) copy-start(f32[3,4,128]{2,1,0:T(4,128)} %get-tuple-element.11) | copy-start | bytes 18436

commit v2 on v1

v2 whole, which is shorter than its diff:
```python
import functools
import math

import jax
import jax.numpy as jnp
from jax import lax
from jax.experimental import pallas as pl
from jax.experimental.pallas import tpu as pltpu
from jax.sharding import PartitionSpec as P

CLUSTER = 16

core_squared = 0.01
step_length = 0.02


def rounded(value):
    return value.astype(jnp.bfloat16).astype(jnp.float32)


def split_three(value):
    one = rounded(value)
    two = rounded(value - one)
    return one, two, rounded(value - one - two)


def split_two(value):
    high = value.astype(jnp.bfloat16)
    return high, (value - high.astype(jnp.float32)).astype(jnp.bfloat16)


def product(left, right):
    return jnp.dot(left, right, preferred_element_type=jnp.float32)


def pad_rows(value):
    return jnp.concatenate([value, jnp.zeros((8 - value.shape[0], value.shape[1]), value.dtype)], axis=0)


def place_parts(state, extra):
    high = rounded(state[0:3])
    low = rounded(state[0:3] - high)
    used = high + low
    norm = used[0:1] * used[0:1] + used[1:2] * used[1:2] + used[2:3] * used[2:3] + extra
    return high, low, split_three(norm)


def source_places(state):
    high, low, norm = place_parts(state, 0.0)
    ones = jnp.ones_like(norm[0])
    none = jnp.zeros_like(norm[0])
    return jnp.concatenate(
        [high, norm[0], norm[1], norm[2], ones, ones]
        + [low, ones, none, none, none, none]
        + [high, none, none, none, none, none]
        + [low, none, none, none, none, none],
        axis=0,
    ).astype(jnp.bfloat16)


def target_places(state):
    high, low, norm = place_parts(state, core_squared)
    high = -2.0 * high
    low = -2.0 * low
    ones = jnp.ones_like(norm[0])
    none = jnp.zeros_like(norm[0])
    return jnp.concatenate(
        [high, ones, ones, ones, norm[0], norm[1]]
        + [high, norm[2], none, none, none, none]
        + [low, none, none, none, none, none]
        + [low, none, none, none, none, none],
        axis=0,
    ).astype(jnp.bfloat16)


def cross(left, right):
    return jnp.concatenate(
        [
            left[1:2] * right[2:3] - left[2:3] * right[1:2],
            left[2:3] * right[0:1] - left[0:1] * right[2:3],
            left[0:1] * right[1:2] - left[1:2] * right[0:1],
        ],
        axis=0,
    )


def source_moments(state):
    base = pad_rows(jnp.concatenate([state[3:6], cross(state[0:3], state[3:6])], axis=0))
    whole = jnp.concatenate([base, state[0:1] * base, state[1:2] * base, state[2:3] * base], axis=0)
    high, low = split_two(whole)
    for_q = jnp.concatenate([high[0:8], low[0:8]], axis=0)
    for_h = jnp.concatenate([high, low], axis=0)
    return for_q, for_h


def pair_sums(places, for_q, for_h, target, both=True):
    length = places.shape[1]
    piece = math.gcd(length, 256)
    parts_q, parts_h = [], []
    left_q, left_h = [], []
    for begin in range(0, length, piece):
        part = slice(begin, begin + piece)
        spread = lax.dot_general(
            places[:, part], target, (((0,), (0,)), ((), ())), preferred_element_type=jnp.float32
        )
        inverse = lax.rsqrt(spread)
        square = inverse * inverse
        factor = square * inverse
        steep = factor * square
        if both:
            parts_q.extend(split_two(factor))
            parts_h.extend(split_two(steep))
            left_q.extend([for_q[:, part]] * 2)
            left_h.extend([for_h[:, part]] * 2)
        else:
            parts_q.append(factor.astype(jnp.bfloat16))
            parts_h.append(steep.astype(jnp.bfloat16))
            left_q.append(for_q[:, part])
            left_h.append(for_h[:, part])

    def total(left, right):
        return product(jnp.concatenate(left, axis=1), jnp.concatenate(right, axis=0))

    got_q = total(left_q, parts_q)
    got_h = total(left_h, parts_h)
    return jnp.concatenate([got_q[0:8] + got_q[8:16], got_h[0:32] + got_h[32:64]], axis=0)


def finish(sums, state, coupling):
    places = state[0:3]
    strengths = state[3:6]
    weighted = sums[0:3]
    velocity = cross(places, weighted) - sums[3:6]
    along = (
        strengths[0:1] * places[0:1] + strengths[1:2] * places[1:2] + strengths[2:3] * places[2:3]
    )
    moment = 3.0 * (
        along * sums[8:16]
        - strengths[0:1] * sums[16:24]
        - strengths[1:2] * sums[24:32]
        - strengths[2:3] * sums[32:40]
    )
    stretch = cross(strengths, weighted) - (cross(places, moment[0:3]) - moment[3:6])
    return -coupling * jnp.concatenate([velocity, stretch], axis=0)


def kernel(
    n_t,
    n_s,
    start_ref,
    nodes_ref,
    places_out,
    strengths_out,
    next_places_out,
    next_strengths_out,
    gathered,
    begin,
    sums,
    steps,
    history,
    coarse,
    middles,
    handed,
    pool,
    spots,
    send_a,
    recv_a,
    send_b,
    recv_b,
    send_e,
    recv_e,
    send_w,
    recv_w,
    send_h,
    recv_h,
):
    length = start_ref.shape[1]
    coupling = 1.0 / (4.0 * math.pi * math.sqrt(length * n_s))
    mine = lax.axis_index("tm")
    me = lax.axis_index("space")
    lanes = nodes_ref.shape[1]
    pieces = length // lanes
    rows = 6 * pieces

    def remote(source, target, send, recv, device):
        return pltpu.make_async_remote_copy(
            src_ref=source, dst_ref=target, send_sem=send, recv_sem=recv,
            device_id=device, device_id_type=pl.DeviceIdType.MESH,
        )

    def load(ref, base=0, count=6):
        return jnp.concatenate(
            [ref[pl.ds(base + piece, count, stride=pieces), :] for piece in range(pieces)], axis=1
        )

    def put(ref, base, value):
        for piece in range(pieces):
            ref[pl.ds(base + piece, value.shape[0], stride=pieces), :] = value[
                :, piece * lanes : (piece + 1) * lanes
            ]

    def near(rank):
        left, right = me, n_s - 1 - me
        both_sides = jnp.minimum(left, right)
        inner = rank <= 2 * both_sides
        distance = jnp.where(inner, (rank + 1) // 2, rank - both_sides)
        leftward = jnp.where(inner, rank % 2 == 1, left > right)
        return jnp.where(leftward, me - distance, me + distance)

    peers = [near(rank) for rank in range(1, n_s)]

    barrier = pltpu.get_barrier_semaphore()
    for offset in range(1, n_s):
        pl.semaphore_signal(
            barrier, inc=1, device_id={"space": lax.rem(me + offset, n_s)},
            device_id_type=pl.DeviceIdType.MESH,
        )
    for turn in range(1, n_t):
        for offset in range(n_s):
            pl.semaphore_signal(
                barrier, inc=1,
                device_id={"tm": lax.rem(mine + turn, n_t), "space": lax.rem(me + offset, n_s)},
                device_id_type=pl.DeviceIdType.MESH,
            )
    put(begin.at[me], 0, start_ref[...])
    pl.semaphore_wait(barrier, n_s * n_t - 1)

    def node_copy(peer, slot):
        return remote(nodes_ref, gathered.at[slot], send_a.at[peer], recv_a.at[slot], {"space": peer})

    def start_copy(peer, slot):
        return remote(begin.at[me], begin.at[slot], send_b.at[peer], recv_b.at[slot], {"space": peer})

    for peer in reversed(peers):
        node_copy(peer, me).start()
    for peer in reversed(peers):
        start_copy(peer, me).start()

    total = n_s * length
    clusters = total // CLUSTER
    particle = lax.broadcasted_iota(jnp.int32, (total, clusters), 0)
    cluster = lax.broadcasted_iota(jnp.int32, (total, clusters), 1)
    offset_in = particle - cluster * CLUSTER
    pool[...] = jnp.where((offset_in >= 0) & (offset_in < CLUSTER), 1.0, 0.0).astype(jnp.bfloat16)

    def aggregate(blocks):
        state = pad_rows(jnp.concatenate(blocks, axis=1))
        parts = jnp.concatenate(split_three(state), axis=0).astype(jnp.bfloat16)
        got = jnp.dot(parts, pool[...], preferred_element_type=jnp.float32)
        whole = got[0:8] + got[8:16] + got[16:24]
        return jnp.concatenate([whole[0:3] * (1.0 / CLUSTER), whole[3:6]], axis=0)

    def coarse_sources(blocks):
        merged = aggregate(blocks)
        return (source_places(merged),) + source_moments(merged)

    own = [load(nodes_ref, node * rows) for node in range(3)]
    for node in range(3):
        spots[node] = target_places(own[node])
    for rank in range(n_s):
        if rank > 0:
            source = peers[rank - 1]
            node_copy(source, source).wait_recv()
        for node in range(3):
            if rank > 0:
                state = load(gathered.at[source], node * rows)
            else:
                state = own[node]
            got = pair_sums(source_places(state), *source_moments(state), spots[node], node == 1)
            if rank == 0:
                sums[node] = got
            else:
                sums[node] = sums[node] + got

    def node_blocks(node):
        return [load(nodes_ref, node * rows)] + [load(gathered.at[peer], node * rows) for peer in peers]

    fine = [finish(sums[node], load(nodes_ref, node * rows), coupling) for node in range(3)]

    def coarse_value(blocks, target, both):
        return finish(pair_sums(*coarse_sources(blocks), target_places(target), both), target, coupling)

    coarse_first = coarse_value(node_blocks(0), load(nodes_ref, 0), True)
    put(
        steps.at[mine, me], 0,
        step_length * ((fine[0] + 4.0 * fine[1] + fine[2]) / 6.0 - coarse_first),
    )

    def step_copy(turn, peer, slice_in, place_in):
        return remote(
            steps.at[slice_in, place_in], steps.at[slice_in, place_in],
            send_e.at[turn, peer], recv_e.at[slice_in, place_in], {"tm": turn, "space": peer},
        )

    def hand_out():
        def to_slice(count, carry):
            turn = n_t - 1 - count
            for peer in peers:
                step_copy(turn, peer, mine, me).start()
            step_copy(turn, me, mine, me).start()
            return carry

        lax.fori_loop(0, n_t - 1 - mine, to_slice, 0)
        for peer in peers:
            step_copy(mine, peer, mine, me).start()

    early = n_t // 4

    @pl.when(mine < early)
    def _():
        hand_out()

    def coarse_step(step):
        sources = coarse_sources([history[step, z] for z in range(n_s)])

        def one_block(z, inner):
            state = history[step, z]
            coarse[step, z] = finish(pair_sums(*sources, target_places(state)), state, coupling)
            return inner

        lax.fori_loop(0, n_s, one_block, 0, unroll=math.gcd(n_s, 4))

    def advance(step):
        for z in range(n_s):
            history[step + 1, z] = (
                history[step, z] + step_length * coarse[step, z] + load(steps.at[step, z])
            )

    for peer in peers:
        start_copy(peer, peer).wait_recv()
    for z in range(n_s):
        history[0, z] = load(begin.at[z])
    coarse_last = coarse_value(node_blocks(2), load(nodes_ref, 2 * rows), False)

    @pl.when(mine >= early)
    def _():
        hand_out()

    coarse_step(0)

    def chain_step(step, carry):
        for z in range(n_s):
            step_copy(mine, me, step, z).wait_recv()
        advance(step)
        coarse_step(step + 1)
        return carry

    lax.fori_loop(0, mine, chain_step, 0)
    for peer in peers:
        step_copy(mine, me, mine, peer).wait_recv()
    advance(mine)

    initial = history[mine, me]
    final_state = history[mine + 1, me]
    coarse_end = coarse_value([history[mine + 1, z] for z in range(n_s)], final_state, False)
    change_first = coarse[mine, me] - coarse_first
    change_last = coarse_end - coarse_last
    fixed_first = fine[0] + change_first
    fixed_middle = fine[1] + 0.5 * (change_first + change_last)
    fixed_last = fine[2] + change_last

    def fine_sums(state, spot):
        return pair_sums(source_places(state), *source_moments(state), spot, False)

    spot = target_places(initial)
    got = fine_sums(history[mine, 0], spot)
    for z in range(1, n_s):
        got = got + fine_sums(history[mine, z], spot)
    slope_first = finish(got, initial, coupling)
    sweep_middle = (
        initial
        + 0.5 * step_length * (slope_first - fixed_first)
        + step_length * (5.0 * fixed_first + 8.0 * fixed_middle - fixed_last) / 24.0
    )
    put(middles.at[me], 0, sweep_middle)

    def middle_copy(peer, slot):
        return remote(middles.at[me], middles.at[slot], send_w.at[peer], recv_w.at[slot], {"space": peer})

    for peer in reversed(peers):
        middle_copy(peer, me).start()
    put(places_out, 0, initial[0:3])
    put(strengths_out, 0, initial[3:6])
    put(places_out, 3 * pieces, sweep_middle[0:3])
    put(strengths_out, 3 * pieces, sweep_middle[3:6])
    spot = target_places(sweep_middle)
    sums[1] = fine_sums(sweep_middle, spot)
    for peer in peers:
        middle_copy(peer, peer).wait_recv()
        sums[1] = sums[1] + fine_sums(load(middles.at[peer]), spot)
    slope_middle = finish(sums[1], sweep_middle, coupling)
    sweep_last = (
        sweep_middle
        + 0.5 * step_length * (slope_middle - fixed_middle)
        + step_length * (-fixed_first + 8.0 * fixed_middle + 5.0 * fixed_last) / 24.0
    )
    put(handed.at[0], 0, sweep_last)

    def last_copy():
        return remote(handed.at[0], handed.at[1], send_h, recv_h, {"tm": lax.rem(mine + 1, n_t)})

    @pl.when(mine < n_t - 1)
    def _():
        last_copy().start()

    half = 3 * pieces
    put(places_out, 2 * half, sweep_last[0:3])
    put(strengths_out, 2 * half, sweep_last[3:6])
    for peer in peers:
        node_copy(peer, me).wait_send()
        start_copy(peer, me).wait_send()
        middle_copy(peer, me).wait_send()
        step_copy(mine, peer, mine, me).wait_send()

    def sent(turn, carry):
        for peer in range(n_s):
            step_copy(turn, peer, mine, me).wait_send()
        return carry

    lax.fori_loop(mine + 1, n_t, sent, 0)

    @pl.when(mine == 0)
    def _():
        put(next_places_out, 0, start_ref[0:3])
        put(next_strengths_out, 0, start_ref[3:6])

    @pl.when(mine > 0)
    def _():
        last_copy().wait_recv()
        next_places_out[...] = handed[1, 0:half]
        next_strengths_out[...] = handed[1, half : 2 * half]

    @pl.when(mine < n_t - 1)
    def _():
        last_copy().wait_send()


def pass_on(*refs):
    count = len(refs) // 2
    for source, target in zip(refs[:count], refs[count:]):
        target[...] = source[...]


def solution(mesh):
    n_t, n_s = mesh.shape["tm"], mesh.shape["space"]

    def shards(start_state, fine_nodes):
        length = start_state.shape[1]
        total = length * n_s
        vmem = pl.BlockSpec(memory_space=pltpu.VMEM)
        dma = pltpu.SemaphoreType.DMA
        lanes = math.gcd(length, 128)
        pieces = length // lanes
        results = [
            jax.ShapeDtypeStruct((count * pieces, lanes), jnp.float32) for count in (9, 9, 3, 3)
        ]
        made = pl.pallas_call(
            functools.partial(kernel, n_t, n_s),
            out_shape=tuple(results),
            in_specs=[vmem, vmem],
            out_specs=(vmem, vmem, vmem, vmem),
            scratch_shapes=[
                pltpu.VMEM((n_s, 18 * pieces, lanes), jnp.float32),
                pltpu.VMEM((n_s, 6 * pieces, lanes), jnp.float32),
                pltpu.VMEM((3, 40, length), jnp.float32),
                pltpu.VMEM((n_t, n_s, 6 * pieces, lanes), jnp.float32),
                pltpu.VMEM((n_t + 1, n_s, 6, length), jnp.float32),
                pltpu.VMEM((n_t, n_s, 6, length), jnp.float32),
                pltpu.VMEM((n_s, 6 * pieces, lanes), jnp.float32),
                pltpu.VMEM((2, 6 * pieces, lanes), jnp.float32),
                pltpu.VMEM((total, total // CLUSTER), jnp.bfloat16),
                pltpu.VMEM((3, 32, length), jnp.bfloat16),
                dma((n_s,)), dma((n_s,)),
                dma((n_s,)), dma((n_s,)),
                dma((n_t, n_s)), dma((n_t, n_s)),
                dma((n_s,)), dma((n_s,)),
                dma, dma,
            ],
            compiler_params=pltpu.CompilerParams(collective_id=0, has_side_effects=True),
        )(start_state, fine_nodes.reshape(-1, lanes))
        made = pl.pallas_call(
            pass_on, out_shape=tuple(results), in_specs=[vmem] * 4, out_specs=(vmem,) * 4
        )(*made)
        nodes, ends = (1, 3, 3, length), (1, 3, length)
        return tuple(
            one.reshape(shape) for one, shape in zip(made, (nodes, nodes, ends, ends))
        )

    return jax.shard_map(
        shards,
        mesh=mesh,
        in_specs=(P(None, "space"), P("tm", None, None, "space")),
        out_specs=(
            P("tm", None, None, "space"),
            P("tm", None, None, "space"),
            P("tm", None, "space"),
            P("tm", None, "space"),
        ),
        check_vma=False,
    )
```

time: 47 us -> 46.2 us (0.983)
  the two profiles are of different devices: /device:TPU:7 before, /device:TPU:15 now
where the time goes in v2:
time: 46.2 us; the launch traced here: 45.3 us
  Pallas kernels  41.5 us (90%)
  local copies, waits for them, and re-layouts  3.22 us (7%)
  between operations  0.65 us (1%)
    pallas_call x1, Pallas kernels, shards(): pl.pallas_call(functools.partial(kernel, n_t, n_s), out_shape=tuple(resul...  40.1 us
    reshape x4, local copies, waits for them, and re-layouts, shards(): one.reshape(shape)  3.21 us
    pallas_call x1, Pallas kernels, shards(): pl.pallas_call(pass_on, out_shape=tuple(results), in_specs=[vmem] * 4, ou...  1.37 us

profile of v2, /device:TPU:15, one launch (start us, length us, event | category | flops | bytes accessed | tf_op | source)
XLA Modules:
  0.0 45.3 jit_solution(18270638547683179155)
XLA Ops:
  0.6 40.1 %shard_map.57 = (f32[36,128]{1,0:T(8,128)}, f32[36,128]{1,0:T(8,128)}, f32[12,128]{1,0:T(8,128)}, f32[12,128]{1,0:T(8,128)}) custom-call(f32[6,512]{1,0:T(8,128)} %start_ref.1, f32[72,128]{1,0:T(8,128)} %bitcast.1), custom_call_target="tpu_custom_call" | custom-call | tf_op jit(solution)/shard_map/pallas_call | solution.py:457
  40.7 1.4 %shard_map.58 = (f32[36,128]{1,0:T(8,128)}, f32[36,128]{1,0:T(8,128)}, f32[12,128]{1,0:T(8,128)}, f32[12,128]{1,0:T(8,128)}) custom-call(f32[36,128]{1,0:T(8,128)} %get-tuple-element.12.refs_0_, f32[36,128]{1,0:T(8,128)} %get-tuple-element.13.refs_1_, f32[12,128]{1,0:T(8,128)} %get-tuple-element.14.refs_2_, f32[12,128]{1,0:T(8,128)} %get-tuple-element.15.refs_3_), custom_call_target="tpu_custom_call" | custom-call | tf_op jit(solution)/shard_map/pallas_call | solution.py:481
  42.1 0.0 copy-start.2
  42.1 0.0 copy-start.1
  42.1 1.4 %reshape.28 = f32[1,3,3,512]{3,0,2,1:T(1,128)} reshape(f32[36,128]{1,0:T(8,128)} %get-tuple-element.16) | data formatting | bytes 36864 | tf_op jit(solution)/shard_map/reshape | solution.py:486
  43.5 0.0 copy-done.2
  43.5 0.0 copy-start
  43.5 0.6 %reshape.30 = f32[1,3,512]{2,0,1:T(1,128)} reshape(f32[12,128]{1,0:T(8,128)S(1)} %copy-done.2) | data formatting | bytes 12288 | tf_op jit(solution)/shard_map/reshape | solution.py:486
  44.1 0.0 copy-done.1
  44.1 0.6 %reshape.31 = f32[1,3,512]{2,0,1:T(1,128)} reshape(f32[12,128]{1,0:T(8,128)S(1)} %copy-done.1) | data formatting | bytes 12288 | tf_op jit(solution)/shard_map/reshape | solution.py:486
  44.7 0.0 copy-done
  44.7 0.6 %reshape.29 = f32[1,3,3,512]{3,0,2,1:T(1,128)} reshape(f32[36,128]{1,0:T(8,128)S(1)} %copy-done) | data formatting | bytes 36864 | tf_op jit(solution)/shard_map/reshape | solution.py:486
Async XLA Ops:
  42.1 1.4 %copy-start.2 = (f32[12,128]{1,0:T(8,128)S(1)}, f32[12,128]{1,0:T(8,128)}, u32[]{:S(2)}) copy-start(f32[12,128]{1,0:T(8,128)} %get-tuple-element.18) | copy-start | bytes 18436
  42.1 2.0 %copy-start.1 = (f32[12,128]{1,0:T(8,128)S(1)}, f32[12,128]{1,0:T(8,128)}, u32[]{:S(2)}) copy-start(f32[12,128]{1,0:T(8,128)} %get-tuple-element.19) | copy-start | bytes 18436
  43.5 1.2 %copy-start = (f32[36,128]{1,0:T(8,128)S(1)}, f32[36,128]{1,0:T(8,128)}, u32[]{:S(2)}) copy-start(f32[36,128]{1,0:T(8,128)} %get-tuple-element.17) | copy-start | bytes 55300

commit v3 on v2

v3 whole, which is shorter than its diff:
```python
import functools
import math

import jax
import jax.numpy as jnp
from jax import lax
from jax.experimental import pallas as pl
from jax.experimental.pallas import tpu as pltpu
from jax.sharding import PartitionSpec as P

CLUSTER = 16

core_squared = 0.01
step_length = 0.02


def rounded(value):
    return value.astype(jnp.bfloat16).astype(jnp.float32)


def split_three(value):
    one = rounded(value)
    two = rounded(value - one)
    return one, two, rounded(value - one - two)


def split_two(value):
    high = value.astype(jnp.bfloat16)
    return high, (value - high.astype(jnp.float32)).astype(jnp.bfloat16)


def product(left, right):
    return jnp.dot(left, right, preferred_element_type=jnp.float32)


def cross(left, right):
    return [
        left[1] * right[2] - left[2] * right[1],
        left[2] * right[0] - left[0] * right[2],
        left[0] * right[1] - left[1] * right[0],
    ]


def place_parts(state, extra):
    high = [rounded(one) for one in state[0:3]]
    low = [rounded(one - top) for one, top in zip(state[0:3], high)]
    used = [top + rest for top, rest in zip(high, low)]
    norm = used[0] * used[0] + used[1] * used[1] + used[2] * used[2] + extra
    return high, low, split_three(norm)


SOURCE_ROWS = 56
TARGET_ROWS = 16
SUM_ROWS = 32


def write_rows(ref, first, values, tiles):
    for index, value in enumerate(values):
        ref[(first + index) * tiles : (first + index + 1) * tiles, :] = value


def read_rows(ref, first, count, tiles):
    if tiles == 1:
        return ref[first : first + count, :]
    return jnp.concatenate(
        [ref[pl.ds(first * tiles + tile, count, stride=tiles), :] for tile in range(tiles)], axis=1
    )


def constant_rows(ref, first, count, value, tiles):
    shape = (count * tiles, ref.shape[1])
    ref[first * tiles : (first + count) * tiles, :] = jnp.full(shape, value, jnp.float32)


def prepare_source(ref, tiles):
    constant_rows(ref, 9, 3, 1.0, tiles)
    constant_rows(ref, 12, 4, 0.0, tiles)
    constant_rows(ref, 22, 10, 0.0, tiles)


def prepare_target(ref, tiles):
    constant_rows(ref, 6, 3, 1.0, tiles)
    constant_rows(ref, 12, 4, 0.0, tiles)


def source_operands(ref, state, tiles):
    high, low, norm = place_parts(state, 0.0)
    base = state[3:6] + cross(state[0:3], state[3:6])
    write_rows(ref, 0, high + high + list(norm), tiles)
    write_rows(ref, 16, low + low, tiles)
    write_rows(ref, 32, base, tiles)
    for axis in range(3):
        write_rows(ref, 38 + 6 * axis, [state[axis] * one for one in base], tiles)
    places = read_rows(ref, 0, 32, tiles).astype(jnp.bfloat16)
    moments = read_rows(ref, 32, 24, tiles)
    high = rounded(moments)
    low = moments - high
    for_q = jnp.concatenate([high[0:8], low[0:8]], axis=0).astype(jnp.bfloat16)
    for_h = jnp.concatenate([high, low], axis=0).astype(jnp.bfloat16)
    return places, for_q, for_h


def target_operand(ref, state, tiles):
    high, low, norm = place_parts(state, core_squared)
    write_rows(ref, 0, [-2.0 * one for one in high] + [-2.0 * one for one in low], tiles)
    write_rows(ref, 9, norm, tiles)
    half = read_rows(ref, 0, TARGET_ROWS, tiles).astype(jnp.bfloat16)
    return jnp.concatenate([half, half], axis=0)


def pair_sums(places, for_q, for_h, target, both=True):
    length = places.shape[1]
    piece = math.gcd(length, 256)
    parts_q, parts_h = [], []
    left_q, left_h = [], []
    for begin in range(0, length, piece):
        part = slice(begin, begin + piece)
        spread = lax.dot_general(
            places[:, part], target, (((0,), (0,)), ((), ())), preferred_element_type=jnp.float32
        )
        inverse = lax.rsqrt(spread)
        square = inverse * inverse
        factor = square * inverse
        steep = factor * square
        if both:
            parts_q.extend(split_two(factor))
            parts_h.extend(split_two(steep))
            left_q.extend([for_q[:, part]] * 2)
            left_h.extend([for_h[:, part]] * 2)
        else:
            parts_q.append(factor.astype(jnp.bfloat16))
            parts_h.append(steep.astype(jnp.bfloat16))
            left_q.append(for_q[:, part])
            left_h.append(for_h[:, part])

    def total(left, right):
        return product(jnp.concatenate(left, axis=1), jnp.concatenate(right, axis=0))

    got_q = total(left_q, parts_q)
    got_h = total(left_h, parts_h)
    return jnp.concatenate([got_q[0:8] + got_q[8:16], got_h[0:24] + got_h[24:48]], axis=0)


def put_sums(ref, sums, first, tiles):
    lanes = ref.shape[1]
    for tile in range(sums.shape[1] // lanes):
        ref[pl.ds(first + tile, SUM_ROWS, stride=tiles), :] = sums[:, tile * lanes : (tile + 1) * lanes]


def finish(ref, state, coupling, tiles):
    def row(index):
        return ref[index * tiles : (index + 1) * tiles, :]

    places, strengths = state[0:3], state[3:6]
    weighted = [row(index) for index in range(3)]
    turned = cross(places, weighted)
    velocity = [turned[index] - row(3 + index) for index in range(3)]
    along = strengths[0] * places[0] + strengths[1] * places[1] + strengths[2] * places[2]
    moment = [
        3.0
        * (
            along * row(8 + index)
            - strengths[0] * row(14 + index)
            - strengths[1] * row(20 + index)
            - strengths[2] * row(26 + index)
        )
        for index in range(6)
    ]
    bent = cross(places, moment[0:3])
    straight = cross(strengths, weighted)
    stretch = [straight[index] - (bent[index] - moment[3 + index]) for index in range(3)]
    return [-coupling * one for one in velocity + stretch]


def kernel(
    n_t,
    n_s,
    start_ref,
    nodes_ref,
    places_out,
    strengths_out,
    next_places_out,
    next_strengths_out,
    gathered,
    begin,
    sums,
    steps,
    history,
    coarse,
    middles,
    handed,
    pool,
    merged,
    sources,
    targets,
    totals,
    many_source,
    many_target,
    many_total,
    send_a,
    recv_a,
    send_b,
    recv_b,
    send_e,
    recv_e,
    send_w,
    recv_w,
    send_h,
    recv_h,
):
    length = start_ref.shape[1]
    coupling = 1.0 / (4.0 * math.pi * math.sqrt(length * n_s))
    mine = lax.axis_index("tm")
    me = lax.axis_index("space")
    lanes = nodes_ref.shape[1]
    pieces = length // lanes
    rows = 6 * pieces
    tiles = n_s * pieces
    total = n_s * length
    clusters = total // CLUSTER
    cluster_tiles = max(1, clusters // lanes)

    def remote(source, target, send, recv, device):
        return pltpu.make_async_remote_copy(
            src_ref=source, dst_ref=target, send_sem=send, recv_sem=recv,
            device_id=device, device_id_type=pl.DeviceIdType.MESH,
        )

    def comps(ref, base=0):
        return [ref[base + one * pieces : base + (one + 1) * pieces, :] for one in range(6)]

    def flat(ref, base=0):
        return jnp.concatenate(
            [ref[pl.ds(base + piece, 6, stride=pieces), :] for piece in range(pieces)], axis=1
        )

    def near(rank):
        left, right = me, n_s - 1 - me
        both_sides = jnp.minimum(left, right)
        inner = rank <= 2 * both_sides
        distance = jnp.where(inner, (rank + 1) // 2, rank - both_sides)
        leftward = jnp.where(inner, rank % 2 == 1, left > right)
        return jnp.where(leftward, me - distance, me + distance)

    peers = [near(rank) for rank in range(1, n_s)]

    barrier = pltpu.get_barrier_semaphore()
    for offset in range(1, n_s):
        pl.semaphore_signal(
            barrier, inc=1, device_id={"space": lax.rem(me + offset, n_s)},
            device_id_type=pl.DeviceIdType.MESH,
        )
    for turn in range(1, n_t):
        pl.semaphore_signal(
            barrier, inc=1, device_id={"tm": lax.rem(mine + turn, n_t)},
            device_id_type=pl.DeviceIdType.MESH,
        )
    for piece in range(pieces):
        begin[me, pl.ds(piece, 6, stride=pieces), :] = start_ref[:, piece * lanes : (piece + 1) * lanes]
    pl.semaphore_wait(barrier, n_s - 1 + n_t - 1)

    def node_copy(peer, slot):
        return remote(nodes_ref, gathered.at[slot], send_a.at[peer], recv_a.at[slot], {"space": peer})

    def start_copy(peer, slot):
        return remote(begin.at[me], begin.at[slot], send_b.at[peer], recv_b.at[slot], {"space": peer})

    for peer in reversed(peers):
        node_copy(peer, me).start()
    for peer in reversed(peers):
        start_copy(peer, me).start()

    particle = lax.broadcasted_iota(jnp.int32, (total, clusters), 0)
    cluster = lax.broadcasted_iota(jnp.int32, (total, clusters), 1)
    offset_in = particle - cluster * CLUSTER
    pool[...] = jnp.where((offset_in >= 0) & (offset_in < CLUSTER), 1.0, 0.0).astype(jnp.bfloat16)
    for one in range(sources.shape[0]):
        prepare_source(sources.at[one], pieces)
    for one in range(targets.shape[0]):
        prepare_target(targets.at[one], pieces)
    for one in range(many_source.shape[0]):
        prepare_source(many_source.at[one], cluster_tiles)
    prepare_target(many_target, tiles)

    def coarse_sources(blocks, slot):
        state = jnp.concatenate(blocks, axis=1)
        state = jnp.concatenate([state, jnp.zeros((2, state.shape[1]), state.dtype)], axis=0)
        parts = jnp.concatenate(split_three(state), axis=0).astype(jnp.bfloat16)
        got = product(parts, pool[...])
        whole = got[0:8] + got[8:16] + got[16:24]
        if cluster_tiles == 1:
            merged[slot] = whole
        else:
            for tile in range(cluster_tiles):
                merged[slot, pl.ds(tile, 8, stride=cluster_tiles), :] = whole[
                    :, tile * lanes : (tile + 1) * lanes
                ]

        def part(index):
            return merged[slot, index * cluster_tiles : (index + 1) * cluster_tiles, :]

        mean = [part(index) * (1.0 / CLUSTER) for index in range(3)]
        return source_operands(
            many_source.at[slot], mean + [part(index) for index in range(3, 6)], cluster_tiles
        )

    own = [comps(nodes_ref, node * rows) for node in range(3)]
    spots = [target_operand(targets.at[node], own[node], pieces) for node in range(3)]
    for rank in range(n_s):
        if rank > 0:
            source = peers[rank - 1]
            node_copy(source, source).wait_recv()
        for node in range(3):
            state = comps(gathered.at[source], node * rows) if rank > 0 else own[node]
            got = pair_sums(
                *source_operands(sources.at[rank * 3 + node], state, pieces), spots[node], node == 1
            )
            if rank == 0:
                sums[node] = got
            elif rank < n_s - 1:
                sums[node] = sums[node] + got
            else:
                put_sums(totals.at[node], sums[node] + got, 0, pieces)

    def node_blocks(node):
        return [flat(nodes_ref, node * rows)] + [flat(gathered.at[peer], node * rows) for peer in peers]

    fine = [
        finish(totals.at[node], comps(nodes_ref, node * rows), coupling, pieces) for node in range(3)
    ]

    def coarse_value(blocks, slot, spot, state, both):
        put_sums(totals.at[3 + slot], pair_sums(*coarse_sources(blocks, slot), spot, both), 0, pieces)
        return finish(totals.at[3 + slot], state, coupling, pieces)

    coarse_first = coarse_value(node_blocks(0), 0, spots[0], comps(nodes_ref), True)
    for one in range(6):
        steps[mine, me, one * pieces : (one + 1) * pieces, :] = step_length * (
            (fine[0][one] + 4.0 * fine[1][one] + fine[2][one]) / 6.0 - coarse_first[one]
        )

    def step_copy(turn, peer, slice_in, place_in):
        return remote(
            steps.at[slice_in, place_in], steps.at[slice_in, place_in],
            send_e.at[turn, peer], recv_e.at[slice_in, place_in], {"tm": turn, "space": peer},
        )

    def hand_out():
        def to_slice(count, carry):
            turn = n_t - 1 - count
            for peer in peers:
                step_copy(turn, peer, mine, me).start()
            step_copy(turn, me, mine, me).start()
            return carry

        lax.fori_loop(0, n_t - 1 - mine, to_slice, 0)
        for peer in peers:
            step_copy(mine, peer, mine, me).start()

    early = n_t // 4

    @pl.when(mine < early)
    def _():
        hand_out()

    def spread_state(step):
        return [history[step, one * tiles : (one + 1) * tiles, :] for one in range(6)]

    def history_blocks(step):
        return [
            jnp.concatenate(
                [history[step, pl.ds(tile, 6, stride=tiles), :] for tile in range(tiles)], axis=1
            )
        ]

    def coarse_step(step):
        operands = coarse_sources(history_blocks(step), 2)
        state = spread_state(step)
        spot = target_operand(many_target, state, tiles)
        for z in range(n_s):
            got = pair_sums(*operands, spot[:, z * length : (z + 1) * length])
            put_sums(many_total, got, z * pieces, tiles)
        value = finish(many_total, state, coupling, tiles)
        for one in range(6):
            coarse[step, one * tiles : (one + 1) * tiles, :] = value[one]

    def advance(step):
        for one in range(6):
            for z in range(n_s):
                at = one * tiles + z * pieces
                history[step + 1, at : at + pieces, :] = (
                    history[step, at : at + pieces, :]
                    + step_length * coarse[step, at : at + pieces, :]
                    + steps[step, z, one * pieces : (one + 1) * pieces, :]
                )

    def block(ref, step, place):
        return [
            ref[step, pl.ds(one * tiles + place * pieces, pieces), :] for one in range(6)
        ]

    for peer in peers:
        start_copy(peer, peer).wait_recv()
    for z in range(n_s):
        for one in range(6):
            at = one * tiles + z * pieces
            history[0, at : at + pieces, :] = begin[z, one * pieces : (one + 1) * pieces, :]
    coarse_last = coarse_value(node_blocks(2), 1, spots[2], comps(nodes_ref, 2 * rows), False)

    @pl.when(mine >= early)
    def _():
        hand_out()

    coarse_step(0)

    def chain_step(step, carry):
        for z in range(n_s):
            step_copy(mine, me, step, z).wait_recv()
        advance(step)
        coarse_step(step + 1)
        return carry

    lax.fori_loop(0, mine, chain_step, 0)
    for peer in peers:
        step_copy(mine, me, mine, peer).wait_recv()
    advance(mine)

    initial = block(history, mine, me)
    final_state = block(history, mine + 1, me)
    spot = target_operand(targets.at[3], final_state, pieces)
    coarse_end = coarse_value(history_blocks(mine + 1), 3, spot, final_state, False)
    first = block(coarse, mine, me)
    change_first = [first[one] - coarse_first[one] for one in range(6)]
    change_last = [coarse_end[one] - coarse_last[one] for one in range(6)]
    fixed_first = [fine[0][one] + change_first[one] for one in range(6)]
    fixed_middle = [fine[1][one] + 0.5 * (change_first[one] + change_last[one]) for one in range(6)]
    fixed_last = [fine[2][one] + change_last[one] for one in range(6)]

    spot = target_operand(targets.at[4], initial, pieces)
    got = None
    for z in range(n_s):
        state = [history[mine, one * tiles + z * pieces : one * tiles + (z + 1) * pieces, :] for one in range(6)]
        more = pair_sums(*source_operands(sources.at[z], state, pieces), spot, False)
        got = more if got is None else got + more
    put_sums(totals.at[0], got, 0, pieces)
    slope_first = finish(totals.at[0], initial, coupling, pieces)
    sweep_middle = [
        initial[one]
        + 0.5 * step_length * (slope_first[one] - fixed_first[one])
        + step_length * (5.0 * fixed_first[one] + 8.0 * fixed_middle[one] - fixed_last[one]) / 24.0
        for one in range(6)
    ]
    for one in range(6):
        middles[me, one * pieces : (one + 1) * pieces, :] = sweep_middle[one]

    def middle_copy(peer, slot):
        return remote(middles.at[me], middles.at[slot], send_w.at[peer], recv_w.at[slot], {"space": peer})

    for peer in reversed(peers):
        middle_copy(peer, me).start()
    half = 3 * pieces

    def write_out(node, state):
        for one in range(3):
            at = node * half + one * pieces
            places_out[at : at + pieces, :] = state[one]
            strengths_out[at : at + pieces, :] = state[3 + one]

    write_out(0, initial)
    write_out(1, sweep_middle)
    spot = target_operand(targets.at[5], sweep_middle, pieces)
    sums[1] = pair_sums(*source_operands(sources.at[n_s], sweep_middle, pieces), spot, False)
    for rank, peer in enumerate(peers):
        middle_copy(peer, peer).wait_recv()
        got = pair_sums(
            *source_operands(sources.at[n_s + 1 + rank], comps(middles.at[peer]), pieces), spot, False
        )
        if rank < n_s - 2:
            sums[1] = sums[1] + got
        else:
            put_sums(totals.at[1], sums[1] + got, 0, pieces)
    slope_middle = finish(totals.at[1], sweep_middle, coupling, pieces)
    sweep_last = [
        sweep_middle[one]
        + 0.5 * step_length * (slope_middle[one] - fixed_middle[one])
        + step_length * (-fixed_first[one] + 8.0 * fixed_middle[one] + 5.0 * fixed_last[one]) / 24.0
        for one in range(6)
    ]
    for one in range(6):
        handed[0, one * pieces : (one + 1) * pieces, :] = sweep_last[one]

    def last_copy():
        return remote(handed.at[0], handed.at[1], send_h, recv_h, {"tm": lax.rem(mine + 1, n_t)})

    @pl.when(mine < n_t - 1)
    def _():
        last_copy().start()

    write_out(2, sweep_last)
    for peer in peers:
        node_copy(peer, me).wait_send()
        start_copy(peer, me).wait_send()
        middle_copy(peer, me).wait_send()
        step_copy(mine, peer, mine, me).wait_send()

    def sent(turn, carry):
        for peer in range(n_s):
            step_copy(turn, peer, mine, me).wait_send()
        return carry

    lax.fori_loop(mine + 1, n_t, sent, 0)

    @pl.when(mine == 0)
    def _():
        next_places_out[...] = begin[me, 0:half, :]
        next_strengths_out[...] = begin[me, half : 2 * half, :]

    @pl.when(mine > 0)
    def _():
        last_copy().wait_recv()
        next_places_out[...] = handed[1, 0:half]
        next_strengths_out[...] = handed[1, half : 2 * half]

    @pl.when(mine < n_t - 1)
    def _():
        last_copy().wait_send()


def pass_on(*refs):
    count = len(refs) // 2
    for source, target in zip(refs[:count], refs[count:]):
        size = target.shape[1]
        for one in range(target.shape[0]):
            target[one] = source[one * size : (one + 1) * size, :]


def solution(mesh):
    n_t, n_s = mesh.shape["tm"], mesh.shape["space"]

    def shards(start_state, fine_nodes):
        length = start_state.shape[1]
        total = length * n_s
        vmem = pl.BlockSpec(memory_space=pltpu.VMEM)
        dma = pltpu.SemaphoreType.DMA
        lanes = math.gcd(length, 128)
        pieces = length // lanes
        tiles = n_s * pieces
        clusters = total // CLUSTER
        cluster_tiles = max(1, clusters // lanes)
        wide = min(clusters, lanes)

        def scratch(*shape):
            return pltpu.VMEM(shape, jnp.float32)

        made = pl.pallas_call(
            functools.partial(kernel, n_t, n_s),
            out_shape=tuple(
                jax.ShapeDtypeStruct((count * pieces, lanes), jnp.float32) for count in (9, 9, 3, 3)
            ),
            in_specs=[vmem, vmem],
            out_specs=(vmem, vmem, vmem, vmem),
            scratch_shapes=[
                scratch(n_s, 18 * pieces, lanes),
                scratch(n_s, 6 * pieces, lanes),
                scratch(3, SUM_ROWS, length),
                scratch(n_t, n_s, 6 * pieces, lanes),
                scratch(n_t + 1, 6 * tiles, lanes),
                scratch(n_t, 6 * tiles, lanes),
                scratch(n_s, 6 * pieces, lanes),
                scratch(2, 6 * pieces, lanes),
                pltpu.VMEM((total, clusters), jnp.bfloat16),
                scratch(4, 8 * cluster_tiles, wide),
                scratch(3 * n_s, SOURCE_ROWS * pieces, lanes),
                scratch(6, TARGET_ROWS * pieces, lanes),
                scratch(7, SUM_ROWS * pieces, lanes),
                scratch(4, SOURCE_ROWS * cluster_tiles, wide),
                scratch(TARGET_ROWS * tiles, lanes),
                scratch(SUM_ROWS * tiles, lanes),
                dma((n_s,)), dma((n_s,)),
                dma((n_s,)), dma((n_s,)),
                dma((n_t, n_s)), dma((n_t, n_s)),
                dma((n_s,)), dma((n_s,)),
                dma, dma,
            ],
            compiler_params=pltpu.CompilerParams(collective_id=0, has_side_effects=True),
        )(start_state, fine_nodes.reshape(-1, lanes))
        made = pl.pallas_call(
            pass_on,
            out_shape=tuple(
                jax.ShapeDtypeStruct((count, pieces, lanes), jnp.float32) for count in (9, 9, 3, 3)
            ),
            in_specs=[vmem] * 4,
            out_specs=(vmem,) * 4,
        )(*made)
        nodes, ends = (1, 3, 3, length), (1, 3, length)
        return tuple(
            one.reshape(shape) for one, shape in zip(made, (nodes, nodes, ends, ends))
        )

    return jax.shard_map(
        shards,
        mesh=mesh,
        in_specs=(P(None, "space"), P("tm", None, None, "space")),
        out_specs=(
            P("tm", None, None, "space"),
            P("tm", None, None, "space"),
            P("tm", None, "space"),
            P("tm", None, "space"),
        ),
        check_vma=False,
    )
```

time: 46.2 us -> 41.1 us (0.89); the launches traced: 45.3 us -> 40.8 us
  local copies, waits for them, and re-layouts: 3.22 us -> 0 us
  Pallas kernels: 41.5 us -> 40.2 us
    reshape x4 -> x0, local copies, waits for them, and re-layouts: 3.21 us -> none  [shards(): one.reshape(shape)]
    pallas_call x2, Pallas kernels: 41.5 us -> 40.2 us  [the longest x1 38.8 us: shards(): pl.pallas_call(functools.partial(kernel, n_t, n_s), out_shape=tuple((jax....]
where the time goes in v3:
time: 41.1 us; the launch traced here: 40.8 us
  Pallas kernels  40.2 us (98%)
  between operations  0.64 us (2%)
    pallas_call x1, Pallas kernels, shards(): pl.pallas_call(functools.partial(kernel, n_t, n_s), out_shape=tuple((jax....  38.8 us
    pallas_call x1, Pallas kernels, shards(): pl.pallas_call(pass_on, out_shape=tuple((jax.ShapeDtypeStruct((count, pie...  1.37 us

profile of v3, /device:TPU:15, one launch (start us, length us, event | category | flops | bytes accessed | tf_op | source)
XLA Modules:
  0.0 40.8 jit_solution(5305171264054650995)
XLA Ops:
  0.6 38.8 %shard_map.57 = (f32[36,128]{1,0:T(8,128)}, f32[36,128]{1,0:T(8,128)}, f32[12,128]{1,0:T(8,128)}, f32[12,128]{1,0:T(8,128)}) custom-call(f32[6,512]{1,0:T(8,128)} %start_ref.1, f32[72,128]{1,0:T(8,128)} %bitcast.5), custom_call_target="tpu_custom_call" | custom-call | tf_op jit(solution)/shard_map/pallas_call | solution.py:555
  39.5 1.4 %shard_map.58 = (f32[9,4,128]{2,1,0:T(4,128)}, f32[9,4,128]{2,1,0:T(4,128)}, f32[3,4,128]{2,1,0:T(4,128)}, f32[3,4,128]{2,1,0:T(4,128)}) custom-call(f32[36,128]{1,0:T(8,128)} %get-tuple-element.12.refs_0_, f32[36,128]{1,0:T(8,128)} %get-tuple-element.13.refs_1_, f32[12,128]{1,0:T(8,128)} %get-tuple-element.14.refs_2_, f32[12,128]{1,0:T(8,128)} %get-tuple-element.15.refs_3_), custom_call_target="tpu_custom_call" | custom-call | tf_op jit(solution)/shard_map/pallas_call | solution.py:587

commit v4 on v3

--- a/solution.py
+++ b/solution.py
@@ -108,7 +108,70 @@
     return jnp.concatenate([half, half], axis=0)
 
 
+def spread_of(job):
+    return lax.dot_general(
+        job[0], job[3], (((0,), (0,)), ((), ())), preferred_element_type=jnp.float32
+    )
+
+
+def factors_of(job, spread):
+    inverse = lax.rsqrt(spread)
+    square = inverse * inverse
+    factor = square * inverse
+    steep = factor * square
+    if job[4]:
+        return (
+            jnp.concatenate(split_two(factor), axis=0),
+            jnp.concatenate(split_two(steep), axis=0),
+        )
+    return factor.astype(jnp.bfloat16), steep.astype(jnp.bfloat16)
+
+
+def sums_of(job, factors):
+    for_q, for_h = job[1], job[2]
+    if job[4]:
+        for_q = jnp.concatenate([for_q, for_q], axis=1)
+        for_h = jnp.concatenate([for_h, for_h], axis=1)
+    got_q = product(for_q, factors[0])
+    got_h = product(for_h, factors[1])
+    return jnp.concatenate([got_q[0:8] + got_q[8:16], got_h[0:24] + got_h[24:48]], axis=0)
+
+
+def cut(operands, target, both):
+    places, for_q, for_h = operands
+    length = places.shape[1]
+    piece = math.gcd(length, 256)
+    return [
+        (places[:, at : at + piece], for_q[:, at : at + piece], for_h[:, at : at + piece], target, both)
+        for at in range(0, length, piece)
+    ]
+
+
+def run(groups):
+    jobs = [job for group in groups for job in group]
+    spreads, factors, sums = {}, {}, {}
+    for turn in range(len(jobs) + 2):
+        if turn < len(jobs):
+            spreads[turn] = spread_of(jobs[turn])
+        if 0 <= turn - 2:
+            sums[turn - 2] = sums_of(jobs[turn - 2], factors.pop(turn - 2))
+        if 0 <= turn - 1 < len(jobs):
+            factors[turn - 1] = factors_of(jobs[turn - 1], spreads.pop(turn - 1))
+    results, at = [], 0
+    for group in groups:
+        total = sums[at]
+        for more in range(at + 1, at + len(group)):
+            total = total + sums[more]
+        at += len(group)
+        results.append(total)
+    return results
+
+
 def pair_sums(places, for_q, for_h, target, both=True):
+    return run([cut((places, for_q, for_h), target, both)])[0]
+
+
+def whole_sums(places, for_q, for_h, target, both=True):
     length = places.shape[1]
     piece = math.gcd(length, 256)
     parts_q, parts_h = [], []
@@ -229,11 +292,6 @@
     def comps(ref, base=0):
         return [ref[base + one * pieces : base + (one + 1) * pieces, :] for one in range(6)]
 
-    def flat(ref, base=0):
-        return jnp.concatenate(
-            [ref[pl.ds(base + piece, 6, stride=pieces), :] for piece in range(pieces)], axis=1
-        )
-
     def near(rank):
         left, right = me, n_s - 1 - me
         both_sides = jnp.minimum(left, right)
@@ -270,10 +328,13 @@
     for peer in reversed(peers):
         start_copy(peer, me).start()
 
-    particle = lax.broadcasted_iota(jnp.int32, (total, clusters), 0)
-    cluster = lax.broadcasted_iota(jnp.int32, (total, clusters), 1)
-    offset_in = particle - cluster * CLUSTER
-    pool[...] = jnp.where((offset_in >= 0) & (offset_in < CLUSTER), 1.0, 0.0).astype(jnp.bfloat16)
+    per_tile = lanes // CLUSTER
+    inside = lax.broadcasted_iota(jnp.int32, (lanes, lanes), 0) // CLUSTER
+    wanted = lax.broadcasted_iota(jnp.int32, (lanes, lanes), 1) % per_tile
+    pool[...] = jnp.where(inside == wanted, 1.0, 0.0).astype(jnp.bfloat16)
+    tile_of = lax.broadcasted_iota(jnp.int32, (CLUSTER, lanes), 0)
+    owner = lax.broadcasted_iota(jnp.int32, (CLUSTER, lanes), 1) // per_tile
+    merged[...] = jnp.where(tile_of == owner, 1.0, 0.0)
     for one in range(sources.shape[0]):
         prepare_source(sources.at[one], pieces)
     for one in range(targets.shape[0]):
@@ -283,26 +344,32 @@
     prepare_target(many_target, tiles)
 
     def coarse_sources(blocks, slot):
-        state = jnp.concatenate(blocks, axis=1)
-        state = jnp.concatenate([state, jnp.zeros((2, state.shape[1]), state.dtype)], axis=0)
-        parts = jnp.concatenate(split_three(state), axis=0).astype(jnp.bfloat16)
-        got = product(parts, pool[...])
-        whole = got[0:8] + got[8:16] + got[16:24]
-        if cluster_tiles == 1:
-            merged[slot] = whole
-        else:
-            for tile in range(cluster_tiles):
-                merged[slot, pl.ds(tile, 8, stride=cluster_tiles), :] = whole[
-                    :, tile * lanes : (tile + 1) * lanes
-                ]
-
-        def part(index):
-            return merged[slot, index * cluster_tiles : (index + 1) * cluster_tiles, :]
-
-        mean = [part(index) * (1.0 / CLUSTER) for index in range(3)]
-        return source_operands(
-            many_source.at[slot], mean + [part(index) for index in range(3, 6)], cluster_tiles
-        )
+        count = blocks[0].shape[0] // 6
+        parts = [part for block in blocks for part in split_three(block)]
+        got = product(jnp.concatenate(parts, axis=0).astype(jnp.bfloat16), pool[...])
+        size = 6 * count
+        sums = []
+        for at in range(0, got.shape[0], 3 * size):
+            sums.append(got[at : at + size] + got[at + size : at + 2 * size] + got[at + 2 * size : at + 3 * size])
+        state = []
+        for one in range(6):
+            tops = []
+            for first in range(0, tiles, CLUSTER):
+                total_of = None
+                for tile in range(first, min(first + CLUSTER, tiles), min(count, CLUSTER)):
+                    block, inner = sums[tile // count], tile % count
+                    width = min(count, CLUSTER)
+                    shift = tile - first
+                    kept = (
+                        block[one * count + inner : one * count + inner + width]
+                        * merged[shift : shift + width, :]
+                    )
+                    kept = jnp.sum(kept, axis=0, keepdims=True)
+                    total_of = kept if total_of is None else total_of + kept
+                tops.append(total_of)
+            whole = tops[0] if len(tops) == 1 else jnp.concatenate(tops, axis=0)
+            state.append(whole * (1.0 / CLUSTER) if one < 3 else whole)
+        return source_operands(many_source.at[slot], state, cluster_tiles)
 
     own = [comps(nodes_ref, node * rows) for node in range(3)]
     spots = [target_operand(targets.at[node], own[node], pieces) for node in range(3)]
@@ -312,7 +379,7 @@
             node_copy(source, source).wait_recv()
         for node in range(3):
             state = comps(gathered.at[source], node * rows) if rank > 0 else own[node]
-            got = pair_sums(
+            got = whole_sums(
                 *source_operands(sources.at[rank * 3 + node], state, pieces), spots[node], node == 1
             )
             if rank == 0:
@@ -323,7 +390,8 @@
                 put_sums(totals.at[node], sums[node] + got, 0, pieces)
 
     def node_blocks(node):
-        return [flat(nodes_ref, node * rows)] + [flat(gathered.at[peer], node * rows) for peer in peers]
+        part = pl.ds(node * rows, rows)
+        return [nodes_ref[part, :]] + [gathered[peer, part, :] for peer in peers]
 
     fine = [
         finish(totals.at[node], comps(nodes_ref, node * rows), coupling, pieces) for node in range(3)
@@ -367,18 +435,16 @@
         return [history[step, one * tiles : (one + 1) * tiles, :] for one in range(6)]
 
     def history_blocks(step):
-        return [
-            jnp.concatenate(
-                [history[step, pl.ds(tile, 6, stride=tiles), :] for tile in range(tiles)], axis=1
-            )
-        ]
+        return [history[step]]
 
     def coarse_step(step):
         operands = coarse_sources(history_blocks(step), 2)
         state = spread_state(step)
         spot = target_operand(many_target, state, tiles)
-        for z in range(n_s):
-            got = pair_sums(*operands, spot[:, z * length : (z + 1) * length])
+        groups = [
+            cut(operands, spot[:, z * length : (z + 1) * length], True) for z in range(n_s)
+        ]
+        for z, got in enumerate(run(groups)):
             put_sums(many_total, got, z * pieces, tiles)
         value = finish(many_total, state, coupling, tiles)
         for one in range(6):
@@ -440,7 +506,7 @@
     got = None
     for z in range(n_s):
         state = [history[mine, one * tiles + z * pieces : one * tiles + (z + 1) * pieces, :] for one in range(6)]
-        more = pair_sums(*source_operands(sources.at[z], state, pieces), spot, False)
+        more = whole_sums(*source_operands(sources.at[z], state, pieces), spot, False)
         got = more if got is None else got + more
     put_sums(totals.at[0], got, 0, pieces)
     slope_first = finish(totals.at[0], initial, coupling, pieces)
@@ -568,8 +634,8 @@
                 scratch(n_t, 6 * tiles, lanes),
                 scratch(n_s, 6 * pieces, lanes),
                 scratch(2, 6 * pieces, lanes),
-                pltpu.VMEM((total, clusters), jnp.bfloat16),
-                scratch(4, 8 * cluster_tiles, wide),
+                pltpu.VMEM((lanes, lanes), jnp.bfloat16),
+                scratch(CLUSTER, lanes),
                 scratch(3 * n_s, SOURCE_ROWS * pieces, lanes),
                 scratch(6, TARGET_ROWS * pieces, lanes),
                 scratch(7, SUM_ROWS * pieces, lanes),

time: 41.1 us -> 38.4 us (0.934)
  Pallas kernels: 40.2 us -> 37.5 us
    pallas_call x1, Pallas kernels: 38.8 us -> 36.1 us  [shards(): pl.pallas_call(functools.partial(kernel, n_t, n_s), out_shape=tuple((jax....]
where the time goes in v4:
time: 38.4 us; the launch traced here: 38.1 us
  Pallas kernels  37.5 us (98%)
  between operations  0.64 us (2%)
    pallas_call x1, Pallas kernels, shards(): pl.pallas_call(functools.partial(kernel, n_t, n_s), out_shape=tuple((jax....  36.1 us
    pallas_call x1, Pallas kernels, shards(): pl.pallas_call(pass_on, out_shape=tuple((jax.ShapeDtypeStruct((count, pie...  1.37 us

profile of v4, /device:TPU:15, one launch (start us, length us, event | category | flops | bytes accessed | tf_op | source)
XLA Modules:
  0.0 38.1 jit_solution(1436771185894960330)
XLA Ops:
  0.6 36.1 %shard_map.57 = (f32[36,128]{1,0:T(8,128)}, f32[36,128]{1,0:T(8,128)}, f32[12,128]{1,0:T(8,128)}, f32[12,128]{1,0:T(8,128)}) custom-call(f32[6,512]{1,0:T(8,128)} %start_ref.1, f32[72,128]{1,0:T(8,128)} %bitcast.5), custom_call_target="tpu_custom_call" | custom-call | tf_op jit(solution)/shard_map/pallas_call | solution.py:621
  36.8 1.4 %shard_map.58 = (f32[9,4,128]{2,1,0:T(4,128)}, f32[9,4,128]{2,1,0:T(4,128)}, f32[3,4,128]{2,1,0:T(4,128)}, f32[3,4,128]{2,1,0:T(4,128)}) custom-call(f32[36,128]{1,0:T(8,128)} %get-tuple-element.12.refs_0_, f32[36,128]{1,0:T(8,128)} %get-tuple-element.13.refs_1_, f32[12,128]{1,0:T(8,128)} %get-tuple-element.14.refs_2_, f32[12,128]{1,0:T(8,128)} %get-tuple-element.15.refs_3_), custom_call_target="tpu_custom_call" | custom-call | tf_op jit(solution)/shard_map/pallas_call | solution.py:653

commit v5 on v4

--- a/solution.py
+++ b/solution.py
@@ -49,6 +49,7 @@
     return high, low, split_three(norm)
 
 
+SLOTS = 4
 SOURCE_ROWS = 56
 TARGET_ROWS = 16
 SUM_ROWS = 32
@@ -127,13 +128,40 @@
     return factor.astype(jnp.bfloat16), steep.astype(jnp.bfloat16)
 
 
-def sums_of(job, factors):
+def sums_from(job, factors):
     for_q, for_h = job[1], job[2]
     if job[4]:
         for_q = jnp.concatenate([for_q, for_q], axis=1)
         for_h = jnp.concatenate([for_h, for_h], axis=1)
     got_q = product(for_q, factors[0])
     got_h = product(for_h, factors[1])
+    return jnp.concatenate([got_q[0:8] + got_q[8:16], got_h[0:24] + got_h[24:48]], axis=0)
+
+
+def keep_factors(job, spread, kept, slot):
+    inverse = lax.rsqrt(spread)
+    square = inverse * inverse
+    factor = square * inverse
+    steep = factor * square
+    rows = spread.shape[0]
+    if job[4]:
+        for part, value in ((0, factor), (2, steep)):
+            high, low = split_two(value)
+            kept[slot, part * rows : (part + 1) * rows, :] = high
+            kept[slot, (part + 1) * rows : (part + 2) * rows, :] = low
+    else:
+        kept[slot, 0:rows, :] = factor.astype(jnp.bfloat16)
+        kept[slot, 2 * rows : 3 * rows, :] = steep.astype(jnp.bfloat16)
+
+
+def sums_of(job, kept, slot):
+    for_q, for_h = job[1], job[2]
+    rows = for_q.shape[1]
+    if job[4]:
+        for_q = jnp.concatenate([for_q, for_q], axis=1)
+        for_h = jnp.concatenate([for_h, for_h], axis=1)
+    got_q = product(for_q, kept[slot, 0 : for_q.shape[1], :])
+    got_h = product(for_h, kept[slot, 2 * rows : 2 * rows + for_h.shape[1], :])
     return jnp.concatenate([got_q[0:8] + got_q[8:16], got_h[0:24] + got_h[24:48]], axis=0)
 
 
@@ -147,14 +175,34 @@
     ]
 
 
-def run(groups):
+def run(kept, groups):
+    jobs = [job for group in groups for job in group]
+    spreads, sums = {}, {}
+    for turn in range(len(jobs) + 2):
+        if turn < len(jobs):
+            spreads[turn] = spread_of(jobs[turn])
+        if 0 <= turn - 2:
+            sums[turn - 2] = sums_of(jobs[turn - 2], kept, (turn - 2) % SLOTS)
+        if 0 <= turn - 1 < len(jobs):
+            keep_factors(jobs[turn - 1], spreads.pop(turn - 1), kept, (turn - 1) % SLOTS)
+    results, at = [], 0
+    for group in groups:
+        total = sums[at]
+        for more in range(at + 1, at + len(group)):
+            total = total + sums[more]
+        at += len(group)
+        results.append(total)
+    return results
+
+
+def run_values(groups):
     jobs = [job for group in groups for job in group]
     spreads, factors, sums = {}, {}, {}
     for turn in range(len(jobs) + 2):
         if turn < len(jobs):
             spreads[turn] = spread_of(jobs[turn])
         if 0 <= turn - 2:
-            sums[turn - 2] = sums_of(jobs[turn - 2], factors.pop(turn - 2))
+            sums[turn - 2] = sums_from(jobs[turn - 2], factors.pop(turn - 2))
         if 0 <= turn - 1 < len(jobs):
             factors[turn - 1] = factors_of(jobs[turn - 1], spreads.pop(turn - 1))
     results, at = [], 0
@@ -165,10 +213,6 @@
         at += len(group)
         results.append(total)
     return results
-
-
-def pair_sums(places, for_q, for_h, target, both=True):
-    return run([cut((places, for_q, for_h), target, both)])[0]
 
 
 def whole_sums(places, for_q, for_h, target, both=True):
@@ -260,6 +304,7 @@
     many_source,
     many_target,
     many_total,
+    kept,
     send_a,
     recv_a,
     send_b,
@@ -323,7 +368,7 @@
     def start_copy(peer, slot):
         return remote(begin.at[me], begin.at[slot], send_b.at[peer], recv_b.at[slot], {"space": peer})
 
-    for peer in reversed(peers):
+    for peer in peers:
         node_copy(peer, me).start()
     for peer in reversed(peers):
         start_copy(peer, me).start()
@@ -377,11 +422,12 @@
         if rank > 0:
             source = peers[rank - 1]
             node_copy(source, source).wait_recv()
+        groups = []
         for node in range(3):
             state = comps(gathered.at[source], node * rows) if rank > 0 else own[node]
-            got = whole_sums(
-                *source_operands(sources.at[rank * 3 + node], state, pieces), spots[node], node == 1
-            )
+            operands = source_operands(sources.at[rank * 3 + node], state, pieces)
+            groups.append(cut(operands, spots[node], node == 1))
+        for node, got in enumerate(run(kept, groups)):
             if rank == 0:
                 sums[node] = got
             elif rank < n_s - 1:
@@ -398,7 +444,7 @@
     ]
 
     def coarse_value(blocks, slot, spot, state, both):
-        put_sums(totals.at[3 + slot], pair_sums(*coarse_sources(blocks, slot), spot, both), 0, pieces)
+        put_sums(totals.at[3 + slot], whole_sums(*coarse_sources(blocks, slot), spot, both), 0, pieces)
         return finish(totals.at[3 + slot], state, coupling, pieces)
 
     coarse_first = coarse_value(node_blocks(0), 0, spots[0], comps(nodes_ref), True)
@@ -444,7 +490,7 @@
         groups = [
             cut(operands, spot[:, z * length : (z + 1) * length], True) for z in range(n_s)
         ]
-        for z, got in enumerate(run(groups)):
+        for z, got in enumerate(run_values(groups)):
             put_sums(many_total, got, z * pieces, tiles)
         value = finish(many_total, state, coupling, tiles)
         for one in range(6):
@@ -503,12 +549,14 @@
     fixed_last = [fine[2][one] + change_last[one] for one in range(6)]
 
     spot = target_operand(targets.at[4], initial, pieces)
-    got = None
+    groups = []
     for z in range(n_s):
-        state = [history[mine, one * tiles + z * pieces : one * tiles + (z + 1) * pieces, :] for one in range(6)]
-        more = whole_sums(*source_operands(sources.at[z], state, pieces), spot, False)
-        got = more if got is None else got + more
-    put_sums(totals.at[0], got, 0, pieces)
+        state = [
+            history[mine, one * tiles + z * pieces : one * tiles + (z + 1) * pieces, :]
+            for one in range(6)
+        ]
+        groups.append(cut(source_operands(sources.at[z], state, pieces), spot, False))
+    put_sums(totals.at[0], functools.reduce(jnp.add, run(kept, groups)), 0, pieces)
     slope_first = finish(totals.at[0], initial, coupling, pieces)
     sweep_middle = [
         initial[one]
@@ -535,10 +583,10 @@
     write_out(0, initial)
     write_out(1, sweep_middle)
     spot = target_operand(targets.at[5], sweep_middle, pieces)
-    sums[1] = pair_sums(*source_operands(sources.at[n_s], sweep_middle, pieces), spot, False)
+    sums[1] = whole_sums(*source_operands(sources.at[n_s], sweep_middle, pieces), spot, False)
     for rank, peer in enumerate(peers):
         middle_copy(peer, peer).wait_recv()
-        got = pair_sums(
+        got = whole_sums(
             *source_operands(sources.at[n_s + 1 + rank], comps(middles.at[peer]), pieces), spot, False
         )
         if rank < n_s - 2:
@@ -642,6 +690,7 @@
                 scratch(4, SOURCE_ROWS * cluster_tiles, wide),
                 scratch(TARGET_ROWS * tiles, lanes),
                 scratch(SUM_ROWS * tiles, lanes),
+                pltpu.VMEM((SLOTS, 4 * math.gcd(length, 256), length), jnp.bfloat16),
                 dma((n_s,)), dma((n_s,)),
                 dma((n_s,)), dma((n_s,)),
                 dma((n_t, n_s)), dma((n_t, n_s)),

time: 38.4 us -> 36 us (0.938)
  Pallas kernels: 37.5 us -> 35.1 us
    pallas_call x1, Pallas kernels: 36.1 us -> 33.8 us  [shards(): pl.pallas_call(functools.partial(kernel, n_t, n_s), out_shape=tuple((jax....]
where the time goes in v5:
time: 36 us; the launch traced here: 35.8 us
  Pallas kernels  35.1 us (98%)
  between operations  0.64 us (2%)
    pallas_call x1, Pallas kernels, shards(): pl.pallas_call(functools.partial(kernel, n_t, n_s), out_shape=tuple((jax....  33.8 us
    pallas_call x1, Pallas kernels, shards(): pl.pallas_call(pass_on, out_shape=tuple((jax.ShapeDtypeStruct((count, pie...  1.37 us

profile of v5, /device:TPU:15, one launch (start us, length us, event | category | flops | bytes accessed | tf_op | source)
XLA Modules:
  0.0 35.8 jit_solution(15609408427614354461)
XLA Ops:
  0.6 33.8 %shard_map.57 = (f32[36,128]{1,0:T(8,128)}, f32[36,128]{1,0:T(8,128)}, f32[12,128]{1,0:T(8,128)}, f32[12,128]{1,0:T(8,128)}) custom-call(f32[6,512]{1,0:T(8,128)} %start_ref.1, f32[72,128]{1,0:T(8,128)} %bitcast.5), custom_call_target="tpu_custom_call" | custom-call | tf_op jit(solution)/shard_map/pallas_call | solution.py:669
  34.4 1.4 %shard_map.58 = (f32[9,4,128]{2,1,0:T(4,128)}, f32[9,4,128]{2,1,0:T(4,128)}, f32[3,4,128]{2,1,0:T(4,128)}, f32[3,4,128]{2,1,0:T(4,128)}) custom-call(f32[36,128]{1,0:T(8,128)} %get-tuple-element.12.refs_0_, f32[36,128]{1,0:T(8,128)} %get-tuple-element.13.refs_1_, f32[12,128]{1,0:T(8,128)} %get-tuple-element.14.refs_2_, f32[12,128]{1,0:T(8,128)} %get-tuple-element.15.refs_3_), custom_call_target="tpu_custom_call" | custom-call | tf_op jit(solution)/shard_map/pallas_call | solution.py:702

commit v6 on v5

--- a/solution.py
+++ b/solution.py
@@ -418,6 +418,10 @@
 
     own = [comps(nodes_ref, node * rows) for node in range(3)]
     spots = [target_operand(targets.at[node], own[node], pieces) for node in range(3)]
+    def node_blocks(node):
+        part = pl.ds(node * rows, rows)
+        return [nodes_ref[part, :]] + [gathered[peer, part, :] for peer in peers]
+
     for rank in range(n_s):
         if rank > 0:
             source = peers[rank - 1]
@@ -427,18 +431,18 @@
             state = comps(gathered.at[source], node * rows) if rank > 0 else own[node]
             operands = source_operands(sources.at[rank * 3 + node], state, pieces)
             groups.append(cut(operands, spots[node], node == 1))
+        if rank == n_s - 1:
+            groups.append(cut(coarse_sources(node_blocks(0), 0), spots[0], True))
         for node, got in enumerate(run(kept, groups)):
-            if rank == 0:
+            if node == 3:
+                put_sums(totals.at[3], got, 0, pieces)
+            elif rank == 0:
                 sums[node] = got
             elif rank < n_s - 1:
                 sums[node] = sums[node] + got
             else:
                 put_sums(totals.at[node], sums[node] + got, 0, pieces)
 
-    def node_blocks(node):
-        part = pl.ds(node * rows, rows)
-        return [nodes_ref[part, :]] + [gathered[peer, part, :] for peer in peers]
-
     fine = [
         finish(totals.at[node], comps(nodes_ref, node * rows), coupling, pieces) for node in range(3)
     ]
@@ -447,7 +451,7 @@
         put_sums(totals.at[3 + slot], whole_sums(*coarse_sources(blocks, slot), spot, both), 0, pieces)
         return finish(totals.at[3 + slot], state, coupling, pieces)
 
-    coarse_first = coarse_value(node_blocks(0), 0, spots[0], comps(nodes_ref), True)
+    coarse_first = finish(totals.at[3], comps(nodes_ref), coupling, pieces)
     for one in range(6):
         steps[mine, me, one * pieces : (one + 1) * pieces, :] = step_length * (
             (fine[0][one] + 4.0 * fine[1][one] + fine[2][one]) / 6.0 - coarse_first[one]
@@ -538,16 +542,6 @@
     advance(mine)
 
     initial = block(history, mine, me)
-    final_state = block(history, mine + 1, me)
-    spot = target_operand(targets.at[3], final_state, pieces)
-    coarse_end = coarse_value(history_blocks(mine + 1), 3, spot, final_state, False)
-    first = block(coarse, mine, me)
-    change_first = [first[one] - coarse_first[one] for one in range(6)]
-    change_last = [coarse_end[one] - coarse_last[one] for one in range(6)]
-    fixed_first = [fine[0][one] + change_first[one] for one in range(6)]
-    fixed_middle = [fine[1][one] + 0.5 * (change_first[one] + change_last[one]) for one in range(6)]
-    fixed_last = [fine[2][one] + change_last[one] for one in range(6)]
-
     spot = target_operand(targets.at[4], initial, pieces)
     groups = []
     for z in range(n_s):
@@ -556,7 +550,19 @@
             for one in range(6)
         ]
         groups.append(cut(source_operands(sources.at[z], state, pieces), spot, False))
-    put_sums(totals.at[0], functools.reduce(jnp.add, run(kept, groups)), 0, pieces)
+    final_state = block(history, mine + 1, me)
+    end_spot = target_operand(targets.at[3], final_state, pieces)
+    groups.append(cut(coarse_sources(history_blocks(mine + 1), 3), end_spot, False))
+    *got, end_sums = run(kept, groups)
+    put_sums(totals.at[6], end_sums, 0, pieces)
+    coarse_end = finish(totals.at[6], final_state, coupling, pieces)
+    first = block(coarse, mine, me)
+    change_first = [first[one] - coarse_first[one] for one in range(6)]
+    change_last = [coarse_end[one] - coarse_last[one] for one in range(6)]
+    fixed_first = [fine[0][one] + change_first[one] for one in range(6)]
+    fixed_middle = [fine[1][one] + 0.5 * (change_first[one] + change_last[one]) for one in range(6)]
+    fixed_last = [fine[2][one] + change_last[one] for one in range(6)]
+    put_sums(totals.at[0], functools.reduce(jnp.add, got), 0, pieces)
     slope_first = finish(totals.at[0], initial, coupling, pieces)
     sweep_middle = [
         initial[one]

time: 36 us -> 35.3 us (0.981)
  Pallas kernels: 35.1 us -> 34.4 us
    pallas_call x1, Pallas kernels: 33.8 us -> 33.1 us  [shards(): pl.pallas_call(functools.partial(kernel, n_t, n_s), out_shape=tuple((jax....]
where the time goes in v6:
time: 35.3 us; the launch traced here: 35.1 us
  Pallas kernels  34.4 us (97%)
  between operations  0.64 us (2%)
    pallas_call x1, Pallas kernels, shards(): pl.pallas_call(functools.partial(kernel, n_t, n_s), out_shape=tuple((jax....  33.1 us
    pallas_call x1, Pallas kernels, shards(): pl.pallas_call(pass_on, out_shape=tuple((jax.ShapeDtypeStruct((count, pie...  1.37 us

profile of v6, /device:TPU:15, one launch (start us, length us, event | category | flops | bytes accessed | tf_op | source)
XLA Modules:
  0.0 35.1 jit_solution(8317593311512657476)
XLA Ops:
  0.6 33.1 %shard_map.57 = (f32[36,128]{1,0:T(8,128)}, f32[36,128]{1,0:T(8,128)}, f32[12,128]{1,0:T(8,128)}, f32[12,128]{1,0:T(8,128)}) custom-call(f32[6,512]{1,0:T(8,128)} %start_ref.1, f32[72,128]{1,0:T(8,128)} %bitcast.5), custom_call_target="tpu_custom_call" | custom-call | tf_op jit(solution)/shard_map/pallas_call | solution.py:675
  33.7 1.4 %shard_map.58 = (f32[9,4,128]{2,1,0:T(4,128)}, f32[9,4,128]{2,1,0:T(4,128)}, f32[3,4,128]{2,1,0:T(4,128)}, f32[3,4,128]{2,1,0:T(4,128)}) custom-call(f32[36,128]{1,0:T(8,128)} %get-tuple-element.12.refs_0_, f32[36,128]{1,0:T(8,128)} %get-tuple-element.13.refs_1_, f32[12,128]{1,0:T(8,128)} %get-tuple-element.14.refs_2_, f32[12,128]{1,0:T(8,128)} %get-tuple-element.15.refs_3_), custom_call_target="tpu_custom_call" | custom-call | tf_op jit(solution)/shard_map/pallas_call | solution.py:708
